TPU v7x, 32 devices: a whole 2x2x4 slice. The times are simulated.
32 devices in a mesh: section: 4 (over y, x), ctx: 8 (over z, core).
Axes of the slice: x: 2, y: 2, z: 4, core: 2. Of those that a mesh axis runs over, the one named last changes fastest.
Arguments:
- fwd_in: bfloat16 [4, 1152, 1024], P('section', 'ctx'), may hold values from -6 to 6
- bwd_saved: bfloat16 [4, 1152, 1024], P('section', 'ctx'), may hold values from -6 to 6
- bwd_cot: bfloat16 [4, 1152, 1024], P('section', 'ctx'), may hold values from -6 to 6
- new_tokens: bfloat16 [1024, 1024], P('ctx'), may hold values from -6 to 6
- loss_cot: bfloat16 [1024, 1024], P('ctx'), may hold values from -6 to 6
- gain: bfloat16 [4, 1024], P('section'), may hold values from 0.099609375 to 1.8984375
- w_query: bfloat16 [4, 1024, 1024], P('section'), may hold values from -2 to 2
- w_keyval: bfloat16 [4, 1024, 512], P('section'), may hold values from -2 to 2
- w_out: bfloat16 [4, 1024, 1024], P('section'), may hold values from -0.1875 to 0.1875
Outputs:
- fwd_next: bfloat16 [4, 1152, 1024], P('section', 'ctx')
- cot_next: bfloat16 [4, 1152, 1024], P('section', 'ctx')
All inputs are finite; a program needn't handle non-finite values.
Results may differ from a plain program's by a relative error of at most 0.012.
The roundings to bfloat16 on the way count: a program that leaves them out, or rounds other values in their place, can miss the bound.
Values may be sent and summed in bfloat16 or wider, within the bound.
A program may use at most 64 MiB of HBM per device.

v0:
```python
import jax
import jax.numpy as jnp
from jax import lax
from jax.sharding import PartitionSpec as P

HEADS = 16
KV_HEADS = 4
HEAD_DIM = 64
GROUP = 8


epsilon = 1e-05


def swapped(block, axis, distance):
    count = lax.axis_size(axis)
    route = []
    for low in range(count):
        high = low | 1 << distance
        if high != low and high < count:
            route += [(low, high), (high, low)]
    return lax.ppermute(block, axis, route)


def from_behind(value, axis, steps):
    count = lax.axis_size(axis)
    pairs = [(source, (source + steps) % count) for source in range(count)]
    return lax.ppermute(value, axis, pairs)


def normalize(hidden):
    values = hidden.astype(jnp.float32)
    scale = lax.rsqrt(jnp.mean(values * values, axis=-1, keepdims=True) + epsilon)
    return (values, scale)


def split_heads(query, keyval):
    rows_q = query.shape[0]
    rows_k = keyval.shape[0]
    shared = HEADS // KV_HEADS
    width = KV_HEADS * HEAD_DIM
    grouped = query.reshape(rows_q, KV_HEADS, shared, HEAD_DIM).transpose(1, 2, 0, 3)
    keys = keyval[:, :width].reshape(rows_k, KV_HEADS, HEAD_DIM).transpose(1, 0, 2)
    values = keyval[:, width:].reshape(rows_k, KV_HEADS, HEAD_DIM).transpose(1, 0, 2)
    return (grouped, keys, values)


def head_probs(q_head, k_head, allowed):
    scores = jnp.einsum(
        "grd,kd->grk", q_head, k_head, preferred_element_type=jnp.float32
    ) * HEAD_DIM ** (-0.5)
    scores = jnp.where(allowed[None], scores, -1e30)
    top = jnp.max(scores, axis=-1, keepdims=True)
    expd = jnp.exp(scores - top)
    return expd / jnp.sum(expd, axis=-1, keepdims=True)


def attend_forward(query, keyval, allowed):
    grouped, keys, values = split_heads(query, keyval)

    def one_head(items):
        q_head, k_head, v_head = items
        weights = head_probs(q_head, k_head, allowed).astype(jnp.bfloat16)
        return jnp.einsum("grk,kd->grd", weights, v_head, preferred_element_type=jnp.float32)

    outs = lax.map(one_head, (grouped, keys, values))
    return outs.transpose(2, 0, 1, 3).reshape(query.shape[0], HEADS * HEAD_DIM).astype(jnp.bfloat16)


def attend_backward(query, keyval, allowed, grad_mixed):
    grouped, keys, values = split_heads(query, keyval)
    shared = HEADS // KV_HEADS
    grads = grad_mixed.reshape(query.shape[0], KV_HEADS, shared, HEAD_DIM).transpose(1, 2, 0, 3)

    def one_head(items):
        q_head, k_head, v_head, g_head = items
        probs = head_probs(q_head, k_head, allowed)
        weights = probs.astype(jnp.bfloat16)
        dprobs = jnp.einsum("grd,kd->grk", g_head, v_head, preferred_element_type=jnp.float32)
        delta = jnp.sum(dprobs * probs, axis=-1, keepdims=True)
        dscores = (probs * (dprobs - delta) * HEAD_DIM ** (-0.5)).astype(jnp.bfloat16)
        grad_q = jnp.einsum("grk,kd->grd", dscores, k_head, preferred_element_type=jnp.float32)
        grad_k = jnp.einsum("grk,grd->kd", dscores, q_head, preferred_element_type=jnp.float32)
        grad_v = jnp.einsum("grk,grd->kd", weights, g_head, preferred_element_type=jnp.float32)
        return (grad_q, grad_k, grad_v)

    grad_q, grad_k, grad_v = lax.map(one_head, (grouped, keys, values, grads))
    rows_k = keyval.shape[0]
    grad_query = (
        grad_q.transpose(2, 0, 1, 3).reshape(query.shape[0], HEADS * HEAD_DIM).astype(jnp.bfloat16)
    )
    grad_keys = grad_k.transpose(1, 0, 2).reshape(rows_k, KV_HEADS * HEAD_DIM)
    grad_values = grad_v.transpose(1, 0, 2).reshape(rows_k, KV_HEADS * HEAD_DIM)
    return (grad_query, jnp.concatenate([grad_keys, grad_values], axis=1))


def project(hidden, gain_row, w_query, w_keyval):
    values, scale = normalize(hidden)
    normed = (values * scale * gain_row.astype(jnp.float32)).astype(jnp.bfloat16)
    query = jnp.dot(normed, w_query, preferred_element_type=jnp.float32).astype(jnp.bfloat16)
    keyval = jnp.dot(normed, w_keyval, preferred_element_type=jnp.float32).astype(jnp.bfloat16)
    return (values, scale, query, keyval)


def bit_order():
    count = GROUP.bit_length() - 1
    return list(range(count - 1, -1, -1))


def collect_pairs(piece, member):
    count = GROUP.bit_length() - 1
    bit_list = bit_order()
    stacked = piece[None]
    for place in bit_list:
        partner = swapped(stacked, "ctx", place)
        upper = member // 2**place % 2
        stacked = jnp.where(
            upper == 0,
            jnp.concatenate([stacked, partner], axis=0),
            jnp.concatenate([partner, stacked], axis=0),
        )
    axes_bits = [bit_list[count - 1 - level] for level in range(count)]
    layout = [axes_bits.index(count - 1 - level) for level in range(count)]
    shaped = stacked.reshape([2] * count + list(piece.shape))
    shaped = shaped.transpose(layout + [count, count + 1])
    return shaped.reshape(GROUP * piece.shape[0], piece.shape[1])


def reduce_pairs(terms, member):
    count = GROUP.bit_length() - 1
    shaped = terms.reshape([2] * count + list(terms.shape[1:]))
    axes_bits = list(range(count - 1, -1, -1))
    for place in bit_order():
        axis = axes_bits.index(place)
        upper = member // 2**place % 2
        low_half = lax.index_in_dim(shaped, 0, axis, keepdims=False)
        high_half = lax.index_in_dim(shaped, 1, axis, keepdims=False)
        keep = jnp.where(upper == 0, low_half, high_half)
        give = jnp.where(upper == 0, high_half, low_half)
        shaped = keep + swapped(give.astype(jnp.bfloat16), "ctx", place).astype(give.dtype)
        axes_bits = [other for other in axes_bits if other != place]
    return shaped


def shards(fwd_in, bwd_saved, bwd_cot, new_tokens, loss_cot, gain, w_query, w_keyval, w_out):
    member = lax.axis_index("ctx") % GROUP
    section_now = lax.axis_index("section")
    section_count = lax.axis_size("section")
    rows_dev = fwd_in.shape[1]
    seg_dev = new_tokens.shape[0]
    mem_dev = rows_dev - seg_dev
    gain_row = gain[0]
    wq_layer = w_query[0]
    wkv_layer = w_keyval[0]
    wo_layer = w_out[0]
    collect, reduce_back = (collect_pairs, reduce_pairs)
    inner = jnp.arange(rows_dev, dtype=jnp.int32)
    query_memory = inner < mem_dev
    query_position = member * seg_dev + inner - mem_dev
    key_rows = jnp.arange(GROUP * rows_dev, dtype=jnp.int32)
    key_inner = key_rows % rows_dev
    key_memory = key_inner < mem_dev
    key_position = key_rows // rows_dev * seg_dev + key_inner - mem_dev
    allowed = (
        key_memory[None, :]
        | query_memory[:, None]
        | (key_position[None, :] <= query_position[:, None])
    )
    values, scale, query, keyval = project(fwd_in[0], gain_row, wq_layer, wkv_layer)
    keyval_all = collect(keyval, member)
    mixed = attend_forward(query, keyval_all, allowed)
    layer_out = (values + jnp.dot(mixed, wo_layer, preferred_element_type=jnp.float32)).astype(
        jnp.bfloat16
    )
    arrived = from_behind(layer_out, "section", 1)
    head_rows = jnp.concatenate([arrived[:mem_dev], new_tokens], axis=0)
    fwd_next = jnp.where(section_now == 0, head_rows, arrived)[None]
    grad_out = bwd_cot[0]
    saved_values, saved_scale, saved_query, saved_keyval = project(
        bwd_saved[0], gain_row, wq_layer, wkv_layer
    )
    saved_all = collect(saved_keyval, member)
    grad_mixed = jnp.einsum(
        "rd,fd->rf", grad_out, wo_layer, preferred_element_type=jnp.float32
    ).astype(jnp.bfloat16)
    grad_query, grad_kv = attend_backward(saved_query, saved_all, allowed, grad_mixed)
    terms = grad_kv.reshape(GROUP, rows_dev, grad_kv.shape[1])
    grad_keyval = reduce_back(terms, member).astype(jnp.bfloat16)
    grad_normed = jnp.einsum("rf,df->rd", grad_query, wq_layer, preferred_element_type=jnp.float32)
    grad_normed = grad_normed + jnp.einsum(
        "rf,df->rd", grad_keyval, wkv_layer, preferred_element_type=jnp.float32
    )
    plain = saved_values * saved_scale
    pushed = gain_row.astype(jnp.float32) * grad_normed
    grad_in = grad_out.astype(jnp.float32) + saved_scale * (
        pushed - plain * jnp.mean(pushed * plain, axis=-1, keepdims=True)
    )
    grad_in = grad_in.astype(jnp.bfloat16)
    returned = from_behind(grad_in, "section", -1)
    tail_rows = jnp.concatenate([returned[:mem_dev], loss_cot], axis=0)
    cot_next = jnp.where(section_now == section_count - 1, tail_rows, returned)[None]
    return (fwd_next, cot_next)


def solution(mesh):
    return jax.shard_map(
        shards,
        mesh=mesh,
        in_specs=(
            P("section", "ctx", None),
            P("section", "ctx", None),
            P("section", "ctx", None),
            P("ctx", None),
            P("ctx", None),
            P("section", None),
            P("section", None, None),
            P("section", None, None),
            P("section", None, None),
        ),
        out_specs=(P("section", "ctx", None), P("section", "ctx", None)),
        check_vma=False,
    )
```

profile of v0, /device:TPU:11, one launch (start us, length us, event | category | flops | bytes accessed | tf_op | source)
XLA Modules:
  0.0 225.6 jit_solution(8824010599595770159)
XLA Ops:
  1.5 1.3 fusion.167
  2.9 1.7 fusion.150
  4.6 2.4 %collective-permute-start.4 = (bf16[1,144,512]{2,1,0:T(8,128)(2,1)S(1)}, bf16[1,144,512]{2,1,0:T(8,128)(2,1)}, u32[]{:S(2)}, u32[]{:S(2)}) collective-permute-start(bf16[1,144,512]{2,1,0:T(8,128)(2,1)S(1)} %fusion.150), channel_id=1, source_target_pairs={{0,4},{4,0},{1,5},{5,1},{2,6},{6,2},{3,7},{7,3},{8,12},{12,8},{9,1... | collective-permute-start | bytes 442376 | tf_op jit(solution)/shard_map/ppermute | solution.py:22
  8.7 1.2 fusion.142
  9.9 6.8 %collective-permute-done.4 = bf16[1,144,512]{2,1,0:T(8,128)(2,1)} collective-permute-done((bf16[1,144,512]{2,1,0:T(8,128)(2,1)S(1)}, bf16[1,144,512]{2,1,0:T(8,128)(2,1)}, u32[]{:S(2)}, u32[]{:S(2)}) %collective-permute-start.4) | collective-permute-done | bytes 147488 | tf_op jit(solution)/shard_map/ppermute | solution.py:22
  16.7 1.2 maximum_select_fusion.6
  18.2 1.6 fusion.145
  19.7 1.2 fusion.139
  21.0 4.6 %collective-permute-done.5 = bf16[2,144,512]{2,1,0:T(8,128)(2,1)} collective-permute-done((bf16[2,144,512]{2,1,0:T(8,128)(2,1)S(1)}, bf16[2,144,512]{2,1,0:T(8,128)(2,1)}, u32[]{:S(2)}, u32[]{:S(2)}) %collective-permute-start.5) | collective-permute-done | bytes 294944 | tf_op jit(solution)/shard_map/ppermute | solution.py:22
  26.8 2.0 collective-permute-start.6
  28.7 1.4 reshape.195
  30.1 1.5 copy.51
  31.6 2.2 reshape.198
  33.8 1.4 copy.52
  35.2 2.2 reshape.191
  37.4 2.1 copy.47
  41.0 8.1 %collective-permute-done.1 = bf16[2,144,512]{2,1,0:T(8,128)(2,1)S(1)} collective-permute-done((bf16[2,144,512]{2,1,0:T(8,128)(2,1)S(1)}, bf16[2,144,512]{2,1,0:T(8,128)(2,1)S(1)}, u32[]{:S(2)}, u32[]{:S(2)}) %collective-permute-start.1) | collective-permute-done | bytes 294944 | tf_op jit(solution)/shard_map/ppermute | solution.py:22
  50.9 1.4 maximum_select_fusion.1
  54.5 1.4 copy.50
  56.7 97.6 %while.27 = (s32[]{:T(128)}, bf16[4,4,144,64]{2,3,1,0:T(8,128)(2,1)}, f32[4,1152,64]{1,2,0:T(8,128)}, f32[4,1152,64]{1,2,0:T(8,128)}, bf16[4,4,144,64]{2,3,1,0:T...) while((s32[]{:T(128)}, ...), condition=%wide.region_10.11_spmd.clone, body=%wide.region_6.10_spmd.clone.sunk | while | flops 525373632 | bytes 29172428 | solution.py:87
  57.0 3.6 %fusion.251 = (f32[4,144]{1,0:T(4,128)S(1)}, f32[4,144,1152]{2,1,0:T(8,128)}) fusion(pred[144,1152]{1,0:T(8,128)(4,1)S(1)} %compare_or_fusion.5, bf16[4,1152,64]{1,2,0:T(8,128)(2,1)} %get-tuple-element.447, s32[]{:T(128)} %get-tuple-element.429, bf16[4,4,144,64]{2,3,1,0:T(8,128)(2,1)} %get-tuple-element.446), kind=kOutput, calls=%fused_computation.179.clone.1 | convolution fusion | flops 87590016 | bytes 3101952 | tf_op jit(solution)/shard_map/while/body/eval_jaxpr/sub | solution.py:54
  60.6 2.1 fusion.250
  62.6 7.8 %fusion.253 = f32[4,1152,64]{1,2,0:T(8,128)} fusion(f32[4,1152,64]{1,2,0:T(8,128)} %get-tuple-element.431, s32[]{:T(128)} %get-tuple-element.429, f32[4,144,1152]{2,1,0:T(8,128)} %fusion.250, bf16[4,4,144,64]{2,3,1,0:T(8,128)(2,1)} %get-tuple-element.446, f32[4,144,1152]{2,1,0:T(8,128)} %get-tuple-element.384, f32[4,144]{1,0:T(4,128)S(1)} %get-tuple-element.385), kind=kOutput, calls=%fused_computation.46.clone.1 | convolution fusion | flops 89581248 | bytes 11052032 | tf_op jit(solution)/shard_map/while/body/eval_jaxpr/grk,grd->kd/dot_general | solution.py:83
  70.4 7.5 %fusion.252 = bf16[4,4,144,64]{2,3,1,0:T(8,128)(2,1)} fusion(bf16[4,4,144,64]{2,3,1,0:T(8,128)(2,1)} %get-tuple-element.430, s32[]{:T(128)} %get-tuple-element.429, f32[4,144,1152]{2,1,0:T(8,128)} %fusion.250, bf16[4,1152,64]{1,2,0:T(8,128)(2,1)} %get-tuple-element.447, f32[4,144,1152]{2,1,0:T(8,128)} %get-tuple-element.384, ...), kind=kOutput, calls=%fused_computation.53.clone.1 | convolution fusion | flops 89581248 | bytes 11035648 | tf_op jit(solution)/shard_map/while/body/eval_jaxpr/grk,kd->grd/dot_general | solution.py:82
  77.9 3.2 %fusion.254 = f32[4,1152,64]{1,2,0:T(8,128)} fusion(f32[4,1152,64]{1,2,0:T(8,128)} %get-tuple-element.432, s32[]{:T(128)} %get-tuple-element.429, bf16[4,4,144,64]{2,3,1,0:T(8,128)(2,1)S(1)} %get-tuple-element.448, f32[4,144]{1,0:T(4,128)S(1)} %get-tuple-element.385, pred[144,1152]{1,0:T(8,128)(4,1)S(1)} %compare_or_fusion.5, ...), kind=kOutput, calls=%fused_computation.44.clone.1 | convolution fusion | flops 173188800 | bytes 876544 | tf_op jit(solution)/shard_map/while/body/eval_jaxpr/grk,grd->kd/dot_general | solution.py:84
  81.3 3.6 %fusion.251 = (f32[4,144]{1,0:T(4,128)S(1)}, f32[4,144,1152]{2,1,0:T(8,128)}) fusion(pred[144,1152]{1,0:T(8,128)(4,1)S(1)} %compare_or_fusion.5, bf16[4,1152,64]{1,2,0:T(8,128)(2,1)} %get-tuple-element.447, s32[]{:T(128)} %get-tuple-element.429, bf16[4,4,144,64]{2,3,1,0:T(8,128)(2,1)} %get-tuple-element.446), kind=kOutput, calls=%fused_computation.179.clone.1 | convolution fusion | flops 87590016 | bytes 3101952 | tf_op jit(solution)/shard_map/while/body/eval_jaxpr/sub | solution.py:54
  84.9 2.1 fusion.250
  87.0 7.8 %fusion.253 = f32[4,1152,64]{1,2,0:T(8,128)} fusion(f32[4,1152,64]{1,2,0:T(8,128)} %get-tuple-element.431, s32[]{:T(128)} %get-tuple-element.429, f32[4,144,1152]{2,1,0:T(8,128)} %fusion.250, bf16[4,4,144,64]{2,3,1,0:T(8,128)(2,1)} %get-tuple-element.446, f32[4,144,1152]{2,1,0:T(8,128)} %get-tuple-element.384, f32[4,144]{1,0:T(4,128)S(1)} %get-tuple-element.385), kind=kOutput, calls=%fused_computation.46.clone.1 | convolution fusion | flops 89581248 | bytes 11052032 | tf_op jit(solution)/shard_map/while/body/eval_jaxpr/grk,grd->kd/dot_general | solution.py:83
  94.8 7.5 %fusion.252 = bf16[4,4,144,64]{2,3,1,0:T(8,128)(2,1)} fusion(bf16[4,4,144,64]{2,3,1,0:T(8,128)(2,1)} %get-tuple-element.430, s32[]{:T(128)} %get-tuple-element.429, f32[4,144,1152]{2,1,0:T(8,128)} %fusion.250, bf16[4,1152,64]{1,2,0:T(8,128)(2,1)} %get-tuple-element.447, f32[4,144,1152]{2,1,0:T(8,128)} %get-tuple-element.384, ...), kind=kOutput, calls=%fused_computation.53.clone.1 | convolution fusion | flops 89581248 | bytes 11035648 | tf_op jit(solution)/shard_map/while/body/eval_jaxpr/grk,kd->grd/dot_general | solution.py:82
  102.3 3.2 %fusion.254 = f32[4,1152,64]{1,2,0:T(8,128)} fusion(f32[4,1152,64]{1,2,0:T(8,128)} %get-tuple-element.432, s32[]{:T(128)} %get-tuple-element.429, bf16[4,4,144,64]{2,3,1,0:T(8,128)(2,1)S(1)} %get-tuple-element.448, f32[4,144]{1,0:T(4,128)S(1)} %get-tuple-element.385, pred[144,1152]{1,0:T(8,128)(4,1)S(1)} %compare_or_fusion.5, ...), kind=kOutput, calls=%fused_computation.44.clone.1 | convolution fusion | flops 173188800 | bytes 876544 | tf_op jit(solution)/shard_map/while/body/eval_jaxpr/grk,grd->kd/dot_general | solution.py:84
  105.7 3.6 %fusion.251 = (f32[4,144]{1,0:T(4,128)S(1)}, f32[4,144,1152]{2,1,0:T(8,128)}) fusion(pred[144,1152]{1,0:T(8,128)(4,1)S(1)} %compare_or_fusion.5, bf16[4,1152,64]{1,2,0:T(8,128)(2,1)} %get-tuple-element.447, s32[]{:T(128)} %get-tuple-element.429, bf16[4,4,144,64]{2,3,1,0:T(8,128)(2,1)} %get-tuple-element.446), kind=kOutput, calls=%fused_computation.179.clone.1 | convolution fusion | flops 87590016 | bytes 3101952 | tf_op jit(solution)/shard_map/while/body/eval_jaxpr/sub | solution.py:54
  109.4 2.1 fusion.250
  111.4 7.8 %fusion.253 = f32[4,1152,64]{1,2,0:T(8,128)} fusion(f32[4,1152,64]{1,2,0:T(8,128)} %get-tuple-element.431, s32[]{:T(128)} %get-tuple-element.429, f32[4,144,1152]{2,1,0:T(8,128)} %fusion.250, bf16[4,4,144,64]{2,3,1,0:T(8,128)(2,1)} %get-tuple-element.446, f32[4,144,1152]{2,1,0:T(8,128)} %get-tuple-element.384, f32[4,144]{1,0:T(4,128)S(1)} %get-tuple-element.385), kind=kOutput, calls=%fused_computation.46.clone.1 | convolution fusion | flops 89581248 | bytes 11052032 | tf_op jit(solution)/shard_map/while/body/eval_jaxpr/grk,grd->kd/dot_general | solution.py:83
  119.2 7.5 %fusion.252 = bf16[4,4,144,64]{2,3,1,0:T(8,128)(2,1)} fusion(bf16[4,4,144,64]{2,3,1,0:T(8,128)(2,1)} %get-tuple-element.430, s32[]{:T(128)} %get-tuple-element.429, f32[4,144,1152]{2,1,0:T(8,128)} %fusion.250, bf16[4,1152,64]{1,2,0:T(8,128)(2,1)} %get-tuple-element.447, f32[4,144,1152]{2,1,0:T(8,128)} %get-tuple-element.384, ...), kind=kOutput, calls=%fused_computation.53.clone.1 | convolution fusion | flops 89581248 | bytes 11035648 | tf_op jit(solution)/shard_map/while/body/eval_jaxpr/grk,kd->grd/dot_general | solution.py:82
  126.8 3.2 %fusion.254 = f32[4,1152,64]{1,2,0:T(8,128)} fusion(f32[4,1152,64]{1,2,0:T(8,128)} %get-tuple-element.432, s32[]{:T(128)} %get-tuple-element.429, bf16[4,4,144,64]{2,3,1,0:T(8,128)(2,1)S(1)} %get-tuple-element.448, f32[4,144]{1,0:T(4,128)S(1)} %get-tuple-element.385, pred[144,1152]{1,0:T(8,128)(4,1)S(1)} %compare_or_fusion.5, ...), kind=kOutput, calls=%fused_computation.44.clone.1 | convolution fusion | flops 173188800 | bytes 876544 | tf_op jit(solution)/shard_map/while/body/eval_jaxpr/grk,grd->kd/dot_general | solution.py:84
  130.2 3.6 %fusion.251 = (f32[4,144]{1,0:T(4,128)S(1)}, f32[4,144,1152]{2,1,0:T(8,128)}) fusion(pred[144,1152]{1,0:T(8,128)(4,1)S(1)} %compare_or_fusion.5, bf16[4,1152,64]{1,2,0:T(8,128)(2,1)} %get-tuple-element.447, s32[]{:T(128)} %get-tuple-element.429, bf16[4,4,144,64]{2,3,1,0:T(8,128)(2,1)} %get-tuple-element.446), kind=kOutput, calls=%fused_computation.179.clone.1 | convolution fusion | flops 87590016 | bytes 3101952 | tf_op jit(solution)/shard_map/while/body/eval_jaxpr/sub | solution.py:54
  133.8 2.1 fusion.250
  135.8 7.8 %fusion.253 = f32[4,1152,64]{1,2,0:T(8,128)} fusion(f32[4,1152,64]{1,2,0:T(8,128)} %get-tuple-element.431, s32[]{:T(128)} %get-tuple-element.429, f32[4,144,1152]{2,1,0:T(8,128)} %fusion.250, bf16[4,4,144,64]{2,3,1,0:T(8,128)(2,1)} %get-tuple-element.446, f32[4,144,1152]{2,1,0:T(8,128)} %get-tuple-element.384, f32[4,144]{1,0:T(4,128)S(1)} %get-tuple-element.385), kind=kOutput, calls=%fused_computation.46.clone.1 | convolution fusion | flops 89581248 | bytes 11052032 | tf_op jit(solution)/shard_map/while/body/eval_jaxpr/grk,grd->kd/dot_general | solution.py:83
  143.7 7.5 %fusion.252 = bf16[4,4,144,64]{2,3,1,0:T(8,128)(2,1)} fusion(bf16[4,4,144,64]{2,3,1,0:T(8,128)(2,1)} %get-tuple-element.430, s32[]{:T(128)} %get-tuple-element.429, f32[4,144,1152]{2,1,0:T(8,128)} %fusion.250, bf16[4,1152,64]{1,2,0:T(8,128)(2,1)} %get-tuple-element.447, f32[4,144,1152]{2,1,0:T(8,128)} %get-tuple-element.384, ...), kind=kOutput, calls=%fused_computation.53.clone.1 | convolution fusion | flops 89581248 | bytes 11035648 | tf_op jit(solution)/shard_map/while/body/eval_jaxpr/grk,kd->grd/dot_general | solution.py:82
  151.2 3.2 %fusion.254 = f32[4,1152,64]{1,2,0:T(8,128)} fusion(f32[4,1152,64]{1,2,0:T(8,128)} %get-tuple-element.432, s32[]{:T(128)} %get-tuple-element.429, bf16[4,4,144,64]{2,3,1,0:T(8,128)(2,1)S(1)} %get-tuple-element.448, f32[4,144]{1,0:T(4,128)S(1)} %get-tuple-element.385, pred[144,1152]{1,0:T(8,128)(4,1)S(1)} %compare_or_fusion.5, ...), kind=kOutput, calls=%fused_computation.44.clone.1 | convolution fusion | flops 173188800 | bytes 876544 | tf_op jit(solution)/shard_map/while/body/eval_jaxpr/grk,grd->kd/dot_general | solution.py:84
  154.4 1.6 copy.53
  156.0 2.6 %copy.54 = f32[1152,256]{1,0:T(8,128)} copy(f32[1152,256]{0,1:T(8,128)} %bitcast.271) | data formatting | bytes 2359296 | tf_op jit(solution)/shard_map/reshape | solution.py:93
  158.7 2.2 select_convert_fusion
  160.9 3.2 %collective-permute-start.7 = (bf16[2,2,144,512]{3,2,1,0:T(8,128)(2,1)}, bf16[2,2,144,512]{3,2,1,0:T(8,128)(2,1)}, u32[]{:S(2)}, u32[]{:S(2)}) collective-permute-start(bf16[2,2,144,512]{3,2,1,0:T(8,128)(2,1)} %bitcast.40), channel_id=1, source_target_pairs={{0,4},{4,0},{1,5},{5,1},{2,6},{6,2},{3,7},{7,3},{8,12},{12,8},{9,1... | collective-permute-start | bytes 1769480 | tf_op jit(solution)/shard_map/ppermute | solution.py:22
  164.1 2.0 maximum_select_fusion
  167.2 2.1 copy.45
  169.3 2.1 copy.46
  172.3 22.5 %while.26 = (s32[]{:T(128)}, bf16[4,4,144,64]{2,3,1,0:T(8,128)(2,1)}, bf16[4,4,144,64]{2,3,1,0:T(8,128)(2,1)}, bf16[4,1152,64]{1,2,0:T(8,128)(2,1)}, bf16[4,1152...) while((s32[]{:T(128)}, ...), condition=%wide.region_4.5_spmd.clone, body=%wide.region_1.4_spmd.clone.sunk | while | flops 261276480 | bytes 1478581 | solution.py:66
  172.5 2.2 fusion.236
  174.7 3.3 %fusion.237 = bf16[4,4,144,64]{2,3,1,0:T(8,128)(2,1)} fusion(bf16[4,4,144,64]{2,3,1,0:T(8,128)(2,1)} %get-tuple-element.397, s32[]{:T(128)} %get-tuple-element.396, f32[4,144]{1,0:T(4,128)S(1)} %fusion.236, bf16[4,1152,64]{1,2,0:T(8,128)(2,1)} %get-tuple-element.410, pred[144,1152]{1,0:T(8,128)(4,1)S(1)} %compare_or_fusion.4, ...), kind=kOutput, calls=%fused_computation.10.clone.1 | convolution fusion | flops 173188800 | bytes 858368 | tf_op jit(solution)/shard_map/while/body/eval_jaxpr/grk,kd->grd/dot_general | solution.py:64
  178.1 2.2 fusion.236
  180.3 3.3 %fusion.237 = bf16[4,4,144,64]{2,3,1,0:T(8,128)(2,1)} fusion(bf16[4,4,144,64]{2,3,1,0:T(8,128)(2,1)} %get-tuple-element.397, s32[]{:T(128)} %get-tuple-element.396, f32[4,144]{1,0:T(4,128)S(1)} %fusion.236, bf16[4,1152,64]{1,2,0:T(8,128)(2,1)} %get-tuple-element.410, pred[144,1152]{1,0:T(8,128)(4,1)S(1)} %compare_or_fusion.4, ...), kind=kOutput, calls=%fused_computation.10.clone.1 | convolution fusion | flops 173188800 | bytes 858368 | tf_op jit(solution)/shard_map/while/body/eval_jaxpr/grk,kd->grd/dot_general | solution.py:64
  183.8 2.2 fusion.236
  186.0 3.3 %fusion.237 = bf16[4,4,144,64]{2,3,1,0:T(8,128)(2,1)} fusion(bf16[4,4,144,64]{2,3,1,0:T(8,128)(2,1)} %get-tuple-element.397, s32[]{:T(128)} %get-tuple-element.396, f32[4,144]{1,0:T(4,128)S(1)} %fusion.236, bf16[4,1152,64]{1,2,0:T(8,128)(2,1)} %get-tuple-element.410, pred[144,1152]{1,0:T(8,128)(4,1)S(1)} %compare_or_fusion.4, ...), kind=kOutput, calls=%fused_computation.10.clone.1 | convolution fusion | flops 173188800 | bytes 858368 | tf_op jit(solution)/shard_map/while/body/eval_jaxpr/grk,kd->grd/dot_general | solution.py:64
  189.4 2.2 fusion.236
  191.6 3.3 %fusion.237 = bf16[4,4,144,64]{2,3,1,0:T(8,128)(2,1)} fusion(bf16[4,4,144,64]{2,3,1,0:T(8,128)(2,1)} %get-tuple-element.397, s32[]{:T(128)} %get-tuple-element.396, f32[4,144]{1,0:T(4,128)S(1)} %fusion.236, bf16[4,1152,64]{1,2,0:T(8,128)(2,1)} %get-tuple-element.410, pred[144,1152]{1,0:T(8,128)(4,1)S(1)} %compare_or_fusion.4, ...), kind=kOutput, calls=%fused_computation.10.clone.1 | convolution fusion | flops 173188800 | bytes 858368 | tf_op jit(solution)/shard_map/while/body/eval_jaxpr/grk,kd->grd/dot_general | solution.py:64
  194.8 1.4 broadcast_select_fusion
  196.3 1.3 convert_add_fusion
  198.7 7.4 %collective-permute-done.8 = bf16[2,144,512]{2,1,0:T(8,128)(2,1)S(1)} collective-permute-done((bf16[2,144,512]{2,1,0:T(8,128)(2,1)S(1)}, bf16[2,144,512]{2,1,0:T(8,128)(2,1)S(1)}, u32[]{:S(2)}, u32[]{:S(2)}) %collective-permute-start.8) | collective-permute-done | bytes 294944 | tf_op jit(solution)/shard_map/ppermute | solution.py:22
  206.3 1.2 collective-permute-start.9
  208.0 1.3 collective-permute-start.3
  210.5 6.1 %collective-permute-done.3 = bf16[144,1024]{1,0:T(8,128)(2,1)S(1)} collective-permute-done((bf16[144,1024]{1,0:T(8,128)(2,1)S(1)}, bf16[144,1024]{1,0:T(8,128)(2,1)S(1)}, u32[]{:S(2)}, u32[]{:S(2)}) %collective-permute-start.3) | collective-permute-done | bytes 294944 | tf_op jit(solution)/shard_map/ppermute | solution.py:28
  217.4 6.5 %collective-permute-done.10 = bf16[144,1024]{1,0:T(8,128)(2,1)S(1)} collective-permute-done((bf16[144,1024]{1,0:T(8,128)(2,1)S(1)}, bf16[144,1024]{1,0:T(8,128)(2,1)S(1)}, u32[]{:S(2)}, u32[]{:S(2)}) %collective-permute-start.10) | collective-permute-done | bytes 294944 | tf_op jit(solution)/shard_map/ppermute | solution.py:28
  223.9 1.7 fusion.174
  (81 shorter events, 17.5 us)
Async XLA Ops:
  0.6 8.0 %copy-start = (bf16[1,1024,1024]{2,1,0:T(8,128)(2,1)S(1)}, bf16[1,1024,1024]{2,1,0:T(8,128)(2,1)}, u32[]{:S(2)}) copy-start(bf16[1,1024,1024]{2,1,0:T(8,128)(2,1)} %param.19) | copy-start | bytes 6291460
  0.6 8.0 %copy-start.5 = (bf16[1,144,1024]{2,1,0:T(8,128)(2,1)S(1)}, bf16[1,144,1024]{2,1,0:T(8,128)(2,1)}, u32[]{:S(2)}) copy-start(bf16[1,144,1024]{2,1,0:T(8,128)(2,1)} %param.14) | copy-start | bytes 884740
  0.7 7.4 %copy-start.1 = (bf16[1,1024,512]{2,1,0:T(8,128)(2,1)S(1)}, bf16[1,1024,512]{2,1,0:T(8,128)(2,1)}, u32[]{:S(2)}) copy-start(bf16[1,1024,512]{2,1,0:T(8,128)(2,1)} %param.20) | copy-start | bytes 3145732
  0.7 7.4 %copy-start.7 = (bf16[1,144,1024]{2,1,0:T(8,128)(2,1)S(1)}, bf16[1,144,1024]{2,1,0:T(8,128)(2,1)}, u32[]{:S(2)}) copy-start(bf16[1,144,1024]{2,1,0:T(8,128)(2,1)} %param.13) | copy-start | bytes 884740
  4.6 5.3 %copy-start.13 = (bf16[1,144,512]{2,1,0:T(8,128)(2,1)}, bf16[1,144,512]{2,1,0:T(8,128)(2,1)S(1)}, u32[]{:S(2)}) copy-start(bf16[1,144,512]{2,1,0:T(8,128)(2,1)S(1)} %fusion.150) | copy-start | bytes 442372
  4.6 12.1 %collective-permute-start.4 = (bf16[1,144,512]{2,1,0:T(8,128)(2,1)S(1)}, bf16[1,144,512]{2,1,0:T(8,128)(2,1)}, u32[]{:S(2)}, u32[]{:S(2)}) collective-permute-start(bf16[1,144,512]{2,1,0:T(8,128)(2,1)S(1)} %fusion.150), channel_id=1, source_target_pairs={{0,4},{4,0},{1,5},{5,1},{2,6},{6,2},{3,7},{7,3},{8,12},{12,8},{9,1... | collective-permute-start | bytes 442376 | tf_op jit(solution)/shard_map/ppermute | solution.py:22
  8.1 10.1 %copy-start.11 = (bf16[1,144,1024]{2,1,0:T(8,128)(2,1)S(1)}, bf16[1,144,1024]{2,1,0:T(8,128)(2,1)}, u32[]{:S(2)}) copy-start(bf16[1,144,1024]{2,1,0:T(8,128)(2,1)} %param.15) | copy-start | bytes 884740
  8.5 31.0 %collective-permute-start = (bf16[1,144,512]{2,1,0:T(8,128)(2,1)S(1)}, bf16[1,144,512]{2,1,0:T(8,128)(2,1)}, u32[]{:S(2)}, u32[]{:S(2)}) collective-permute-start(bf16[1,144,512]{2,1,0:T(8,128)(2,1)S(1)} %fusion.149), channel_id=1, source_target_pairs={{0,4},{4,0},{1,5},{5,1},{2,6},{6,2},{3,7},{7,3},{8,12},{12,8},{9,1... | collective-permute-start | bytes 442376 | tf_op jit(solution)/shard_map/ppermute | solution.py:22
  8.6 9.5 %copy-start.3 = (bf16[1,1024,1024]{2,1,0:T(8,128)(2,1)S(1)}, bf16[1,1024,1024]{2,1,0:T(8,128)(2,1)}, u32[]{:S(2)}) copy-start(bf16[1,1024,1024]{2,1,0:T(8,128)(2,1)} %param.21) | copy-start | bytes 6291460
  17.9 7.7 %collective-permute-start.5 = (bf16[2,144,512]{2,1,0:T(8,128)(2,1)S(1)}, bf16[2,144,512]{2,1,0:T(8,128)(2,1)}, u32[]{:S(2)}, u32[]{:S(2)}) collective-permute-start(bf16[2,144,512]{2,1,0:T(8,128)(2,1)S(1)} %maximum_select_fusion.6), channel_id=1, source_target_pairs={{0,2},{2,0},{1,3},{3,1},{4,6},{6,4},{5,7},{7,5},{8,10},{10,8},{9,1... | collective-permute-start | bytes 884744 | tf_op jit(solution)/shard_map/ppermute | solution.py:22
  26.8 24.2 %collective-permute-start.6 = (bf16[4,144,512]{2,1,0:T(8,128)(2,1)S(1)}, bf16[4,144,512]{2,1,0:T(8,128)(2,1)}, u32[]{:S(2)}, u32[]{:S(2)}) collective-permute-start(bf16[4,144,512]{2,1,0:T(8,128)(2,1)S(1)} %maximum_select_fusion.3), channel_id=1, source_target_pairs={{0,1},{1,0},{2,3},{3,2},{4,5},{5,4},{6,7},{7,6},{8,9},{9,8},{10,11... | collective-permute-start | bytes 1769480 | tf_op jit(solution)/shard_map/ppermute | solution.py:22
  40.5 8.6 %collective-permute-start.1 = (bf16[2,144,512]{2,1,0:T(8,128)(2,1)S(1)}, bf16[2,144,512]{2,1,0:T(8,128)(2,1)S(1)}, u32[]{:S(2)}, u32[]{:S(2)}) collective-permute-start(bf16[2,144,512]{2,1,0:T(8,128)(2,1)S(1)} %maximum_select_fusion.4), channel_id=1, source_target_pairs={{0,2},{2,0},{1,3},{3,1},{4,6},{6,4},{5,7},{7,5},{8,10},{10,8},{9,1... | collective-permute-start | bytes 884744 | tf_op jit(solution)/shard_map/ppermute | solution.py:22
  50.0 114.1 %collective-permute-start.2 = (bf16[4,144,512]{2,1,0:T(8,128)(2,1)}, bf16[4,144,512]{2,1,0:T(8,128)(2,1)}, u32[]{:S(2)}, u32[]{:S(2)}) collective-permute-start(bf16[4,144,512]{2,1,0:T(8,128)(2,1)} %maximum_select_fusion.2), channel_id=1, source_target_pairs={{0,1},{1,0},{2,3},{3,2},{4,5},{5,4},{6,7},{7,6},{8,9},{9,8},{10,11... | collective-permute-start | bytes 1769480 | tf_op jit(solution)/shard_map/ppermute | solution.py:22
  160.9 35.4 %collective-permute-start.7 = (bf16[2,2,144,512]{3,2,1,0:T(8,128)(2,1)}, bf16[2,2,144,512]{3,2,1,0:T(8,128)(2,1)}, u32[]{:S(2)}, u32[]{:S(2)}) collective-permute-start(bf16[2,2,144,512]{3,2,1,0:T(8,128)(2,1)} %bitcast.40), channel_id=1, source_target_pairs={{0,4},{4,0},{1,5},{5,1},{2,6},{6,2},{3,7},{7,3},{8,12},{12,8},{9,1... | collective-permute-start | bytes 1769480 | tf_op jit(solution)/shard_map/ppermute | solution.py:22
  196.3 1.5 copy-start.9
  197.7 8.3 %collective-permute-start.8 = (bf16[2,144,512]{2,1,0:T(8,128)(2,1)S(1)}, bf16[2,144,512]{2,1,0:T(8,128)(2,1)S(1)}, u32[]{:S(2)}, u32[]{:S(2)}) collective-permute-start(bf16[2,144,512]{2,1,0:T(8,128)(2,1)S(1)} %fusion.170), channel_id=1, source_target_pairs={{0,2},{2,0},{1,3},{3,1},{4,6},{6,4},{5,7},{7,5},{8,10},{10,8},{9,1... | collective-permute-start | bytes 884744 | tf_op jit(solution)/shard_map/ppermute | solution.py:22
  197.8 9.7 %copy-start.4 = (bf16[1,1024,1024]{2,1,0:T(8,128)(2,1)S(1)}, bf16[1,1024,1024]{2,1,0:T(8,128)(2,1)}, u32[]{:S(2)}) copy-start(bf16[1,1024,1024]{2,1,0:T(8,128)(2,1)} %param.21) | copy-start | bytes 6291460
  197.8 9.7 %copy-start.8 = (bf16[1,144,1024]{2,1,0:T(8,128)(2,1)S(1)}, bf16[1,144,1024]{2,1,0:T(8,128)(2,1)}, u32[]{:S(2)}) copy-start(bf16[1,144,1024]{2,1,0:T(8,128)(2,1)} %param.13) | copy-start | bytes 884740
  197.8 9.7 %copy-start.10 = (bf16[4,4,144,64]{2,3,1,0:T(8,128)(2,1)S(1)}, bf16[4,4,144,64]{2,3,1,0:T(8,128)(2,1)}, u32[]{:S(2)}) copy-start(bf16[4,4,144,64]{2,3,1,0:T(8,128)(2,1)} %get-tuple-element.83) | copy-start | bytes 884740
  206.2 3.1 %copy-start.2 = (bf16[1,1024,512]{2,1,0:T(8,128)(2,1)S(1)}, bf16[1,1024,512]{2,1,0:T(8,128)(2,1)}, u32[]{:S(2)}) copy-start(bf16[1,1024,512]{2,1,0:T(8,128)(2,1)} %param.20) | copy-start | bytes 3145732
  206.2 3.1 %copy-start.6 = (bf16[1,144,1024]{2,1,0:T(8,128)(2,1)S(1)}, bf16[1,144,1024]{2,1,0:T(8,128)(2,1)}, u32[]{:S(2)}) copy-start(bf16[1,144,1024]{2,1,0:T(8,128)(2,1)} %param.14) | copy-start | bytes 884740
  206.3 3.0 %collective-permute-start.9 = (bf16[144,512]{1,0:T(8,128)(2,1)S(1)}, bf16[144,512]{1,0:T(8,128)(2,1)S(1)}, u32[]{:S(2)}, u32[]{:S(2)}) collective-permute-start(bf16[144,512]{1,0:T(8,128)(2,1)S(1)} %fusion.177), channel_id=1, source_target_pairs={{0,1},{1,0},{2,3},{3,2},{4,5},{5,4},{6,7},{7,6},{8,9},{9,8},{10,11... | collective-permute-start | bytes 442376 | tf_op jit(solution)/shard_map/ppermute | solution.py:22
  208.0 1.9 copy-start.12
  208.0 8.6 %copy-start.14 = (bf16[128,1024]{1,0:T(8,128)(2,1)S(1)}, bf16[128,1024]{1,0:T(8,128)(2,1)}, u32[]{:S(2)}) copy-start(bf16[128,1024]{1,0:T(8,128)(2,1)} %param.16) | copy-start | bytes 786436
  208.0 8.6 %collective-permute-start.3 = (bf16[144,1024]{1,0:T(8,128)(2,1)S(1)}, bf16[144,1024]{1,0:T(8,128)(2,1)S(1)}, u32[]{:S(2)}, u32[]{:S(2)}) collective-permute-start(bf16[144,1024]{1,0:T(8,128)(2,1)S(1)} %fusion.136), channel_id=1, source_target_pairs={{0,8},{8,16},{16,24},{24,0},{1,9},{9,17},{17,25},{25,1},{2,10},{10... | collective-permute-start | bytes 884744 | tf_op jit(solution)/shard_map/ppermute | solution.py:28
  210.2 13.7 %collective-permute-start.10 = (bf16[144,1024]{1,0:T(8,128)(2,1)S(1)}, bf16[144,1024]{1,0:T(8,128)(2,1)S(1)}, u32[]{:S(2)}, u32[]{:S(2)}) collective-permute-start(bf16[144,1024]{1,0:T(8,128)(2,1)S(1)} %fusion.163), channel_id=1, source_target_pairs={{0,24},{8,0},{16,8},{24,16},{1,25},{9,1},{17,9},{25,17},{2,26},{10... | collective-permute-start | bytes 884744 | tf_op jit(solution)/shard_map/ppermute | solution.py:28
where the time goes:
time: 228 us; the launch traced here: 226 us
  matrix products  127 us (56%)
  waiting for transfers between devices  39.5 us (17%)
  local copies, waits for them, and re-layouts  25.7 us (11%)
  other arithmetic  20.6 us (9%)
  starting transfers between devices  12.1 us (5%)
    dot_general x4, matrix products, one_head(): jnp.einsum('grk,grd->kd', dscores, q_head, preferred_element_type=jnp.flo...  31.3 us
    dot_general x4, matrix products, one_head(): jnp.einsum('grk,kd->grd', dscores, k_head, preferred_element_type=jnp.flo...  30.1 us
    ppermute x9, waiting for transfers between devices, swapped(): return lax.ppermute(block, axis, route)  27 us
    sub x8, matrix products, head_probs(): expd = jnp.exp(scores - top)  23.1 us
    dot_general x4, matrix products, one_head(): jnp.einsum('grk,kd->grd', weights, v_head, preferred_element_type=jnp.flo...  13 us
    dot_general x4, matrix products, one_head(): jnp.einsum('grk,grd->kd', weights, g_head, preferred_element_type=jnp.flo...  12.8 us
    ppermute x2, waiting for transfers between devices, from_behind(): return lax.ppermute(value, axis, pairs)  12.6 us
    ppermute x9, starting transfers between devices, swapped(): return lax.ppermute(block, axis, route)  10.6 us
  transfers between devices with their start and end apart: 11, of which 6 were waited for; matrix products, arithmetic and copies ran while one was open for 73% of the time, Pallas kernels for 0%

commit v1 on v0

v1 whole, which is shorter than its diff:
```python
import functools

import jax
import jax.numpy as jnp
from jax import lax
from jax.experimental import pallas as pl
from jax.experimental.pallas import tpu as pltpu
from jax.sharding import PartitionSpec as P

HEADS = 16
KV_HEADS = 4
HEAD_DIM = 64
GROUP = 8
PAIR = 2
CHIPS = GROUP // PAIR
LOCAL = KV_HEADS // PAIR
SHARED = HEADS // KV_HEADS
LANES = 128
PIECES = 4

epsilon = 1e-05
far = 1 << 30

bf16 = jnp.bfloat16
f32 = jnp.float32
NT = (((1,), (1,)), ((), ()))
NN = (((1,), (0,)), ((), ()))


def mul(a, b, dims=NN):
    return lax.dot_general(a, b, dims, preferred_element_type=f32)


def kernel(
    sections, mem,
    xf_h, xb_h, cot_h, gain_ref, wq_h, wkv_h, wo_h,
    outf_h, outb_h,
    xf, xb, cot, wq, wkv, wo, normed, kvf, kvb, kvt, qf, qb, gb, kpos,
    sd, ex, cat, acc, gsend, grecv, gsum, stacked, halves, gq_send, gq_all, mix_send, mix_all,
    of, ob,
    local_sem, pair_send, pair_recv, kv_send, kv_recv, gr_send, gr_recv, sec_send, sec_recv,
):
    rows = xf_h.shape[0]
    width = xf_h.shape[1]
    both = PAIR * rows
    total = GROUP * rows
    stack = SHARED * both
    half = width // PAIR
    tokens = rows - mem
    kcols = LOCAL * HEAD_DIM

    ctx = lax.axis_index("ctx")
    section = lax.axis_index("section")
    member = lax.rem(ctx, GROUP)
    base = ctx - member
    core = lax.rem(member, PAIR)
    chip = member // PAIR
    other = 1 - core
    partner = base + chip * PAIR + other

    loads = []
    mine = pl.ds(core * rows, rows)
    for at, (src, dst) in enumerate(
        [
            (xb_h, xb.at[mine]), (wkv_h, wkv), (xf_h, xf.at[mine]),
            (wq_h, wq), (cot_h, cot.at[mine]), (wo_h, wo),
        ]
    ):
        copy = pltpu.make_async_copy(src, dst, local_sem.at[at])
        copy.start()
        loads.append(copy)
    load_xb, load_wkv, load_xf, load_wq, load_cot, load_wo = loads

    after = lax.rem(section + 1, sections)
    before = lax.rem(section + sections - 1, sections)
    barrier = pltpu.get_barrier_semaphore()
    for k in range(1, GROUP):
        pl.semaphore_signal(
            barrier, inc=1, device_id={"ctx": base + lax.rem(member + k, GROUP)},
            device_id_type=pl.DeviceIdType.MESH,
        )
    for neighbour in (after, before):
        pl.semaphore_signal(
            barrier, inc=1, device_id={"section": neighbour},
            device_id_type=pl.DeviceIdType.MESH,
        )
    pl.semaphore_wait(barrier, GROUP + 1)

    def remote(src, dst, send, recv, where):
        return pltpu.make_async_remote_copy(
            src_ref=src, dst_ref=dst, send_sem=send, recv_sem=recv,
            device_id=where, device_id_type=pl.DeviceIdType.MESH,
        )

    theirs = pl.ds(other * rows, rows)

    def pair_copy(at, src, dst):
        copy = remote(src, dst, pair_send.at[at], pair_recv.at[at], {"ctx": partner})
        copy.start()
        return copy

    pair_copies = [
        pair_copy(0, xb_h, xb.at[mine]),
        pair_copy(1, xf_h, xf.at[mine]),
        pair_copy(2, cot_h, cot.at[mine]),
    ]

    def pair_arrived(at, dst):
        remote(dst, dst, pair_send.at[at], pair_recv.at[at], {"ctx": partner}).wait_recv()

    for b in range(GROUP):
        inner = lax.broadcasted_iota(jnp.int32, (rows, LANES), 0)
        kpos[b * rows : (b + 1) * rows, :] = jnp.where(
            inner < mem, -1, b * tokens + inner - mem
        )

    gain = gain_ref[...].astype(f32)

    def norm(x):
        values = x.astype(f32)
        scale = lax.rsqrt(jnp.mean(values * values, axis=-1, keepdims=True) + epsilon)
        return values, scale

    def make_normed(x_ref):
        for b in range(PAIR):
            values, scale = norm(x_ref[b * rows : (b + 1) * rows, :])
            normed[b * rows : (b + 1) * rows, :] = (values * scale * gain).astype(bf16)

    chip_rows = pl.ds(chip * both, both)

    def project_kv(kv_ref, kind):
        keys = mul(normed[...], wkv[:, pl.ds(pl.multiple_of(core * kcols, kcols), kcols)])
        vals = mul(
            normed[...],
            wkv[:, pl.ds(pl.multiple_of(KV_HEADS * HEAD_DIM + core * kcols, kcols), kcols)],
        )
        for g in range(LOCAL):
            lanes = slice(g * HEAD_DIM, (g + 1) * HEAD_DIM)
            kv_ref[g, chip_rows, :] = jnp.concatenate(
                [keys[:, lanes], vals[:, lanes]], axis=1
            ).astype(bf16)
        copies = []
        for g in range(LOCAL):
            for k in range(1, CHIPS):
                to = base + lax.rem(chip + k, CHIPS) * PAIR + core
                copy = remote(
                    kv_ref.at[g, chip_rows], kv_ref.at[g, chip_rows],
                    kv_send.at[kind, g, k], kv_recv.at[kind, g, k], {"ctx": to},
                )
                copy.start()
                copies.append(copy)
        return copies

    def kv_arrived(kv_ref, kind, g):
        for k in range(1, CHIPS):
            source = lax.rem(chip + CHIPS - k, CHIPS)
            place = kv_ref.at[g, pl.ds(source * both, both)]
            remote(
                place, place, kv_send.at[kind, g, k], kv_recv.at[kind, g, k],
                {"ctx": base + source * PAIR + core},
            ).wait_recv()

    def spread(matrix, dst, upper, factor):
        rounded = matrix.astype(bf16).astype(f32) * factor
        zero = jnp.zeros((both, HEAD_DIM), f32)
        for g in range(LOCAL):
            for h in range(SHARED):
                at = (g * SHARED + h) * HEAD_DIM
                piece = rounded[:, at : at + HEAD_DIM]
                parts = [zero, piece] if upper else [piece, zero]
                dst[g, h * both : (h + 1) * both, :] = jnp.concatenate(parts, axis=1).astype(bf16)

    scale_by = HEAD_DIM ** (-0.5)
    my_cols = pl.ds(pl.multiple_of(core * half, half), half)

    load_xb.wait()
    pair_arrived(0, xb.at[theirs])
    make_normed(xb)
    load_wkv.wait()
    kv_copies = project_kv(kvb, 0)
    load_wq.wait()
    spread(mul(normed[...], wq[:, my_cols]), qb, False, scale_by)
    load_xf.wait()
    pair_arrived(1, xf.at[theirs])
    make_normed(xf)
    kv_copies += project_kv(kvf, 1)
    load_cot.wait()
    pair_arrived(2, cot.at[theirs])
    load_wo.wait()
    spread(mul(cot[...], wo[my_cols, :], NT), gb, True, 1.0)
    spread(mul(normed[...], wq[:, my_cols]), qf, False, scale_by)

    step = total // PIECES

    def query_positions(start):
        row = start + lax.broadcasted_iota(jnp.int32, (1, LANES), 1)
        for h in range(1, SHARED):
            row = jnp.where(row >= both, row - both, row)
        block = jnp.where(row >= rows, 1, 0)
        inner = row - block * rows
        return jnp.where(inner < mem, far, (chip * PAIR + block) * tokens + inner - mem)

    def backward_chunk(g, i, carry):
        start = pl.multiple_of(i * LANES, LANES)
        pair = jnp.concatenate([qb[g, pl.ds(start, LANES), :], gb[g, pl.ds(start, LANES), :]], axis=0)
        position = query_positions(start)
        top = None
        for p in range(PIECES):
            part = slice(p * step, (p + 1) * step)
            product = mul(kvb[g, part, :], pair, NT)
            scores = jnp.where(kpos[part, :] <= position, product[:, :LANES], -1e30)
            sd[part, :LANES] = scores
            sd[part, LANES:] = product[:, LANES:]
            peak = jnp.max(scores, axis=0, keepdims=True)
            top = peak if top is None else jnp.maximum(top, peak)
        norm_sum = jnp.zeros((1, LANES), f32)
        delta = jnp.zeros((1, LANES), f32)
        for p in range(PIECES):
            part = slice(p * step, (p + 1) * step)
            expd = jnp.exp(sd[part, :LANES] - top)
            ex[part, :] = expd
            norm_sum += jnp.sum(expd, axis=0, keepdims=True)
            delta += jnp.sum(expd * sd[part, LANES:], axis=0, keepdims=True)
        inverse = 1.0 / norm_sum
        delta = delta * inverse
        for p in range(PIECES):
            part = slice(p * step, (p + 1) * step)
            probs = ex[part, :] * inverse
            cat[part, LANES:] = probs.astype(bf16)
            cat[part, :LANES] = (probs * (sd[part, LANES:] - delta)).astype(bf16)
            acc[g, part, :] += mul(cat[part, :], pair)
        turned = mul(kvt[...], cat[:, :LANES])
        stacked[g, pl.ds(start, LANES), :] = turned.T * scale_by
        return carry

    def forward_chunk(g, i, carry):
        start = pl.multiple_of(i * LANES, LANES)
        queries = qf[g, pl.ds(start, LANES), :]
        position = query_positions(start)
        top = None
        for p in range(PIECES):
            part = slice(p * step, (p + 1) * step)
            product = mul(kvf[g, part, :], queries, NT)
            scores = jnp.where(kpos[part, :] <= position, product, -1e30)
            sd[part, :LANES] = scores
            peak = jnp.max(scores, axis=0, keepdims=True)
            top = peak if top is None else jnp.maximum(top, peak)
        norm_sum = jnp.zeros((1, LANES), f32)
        for p in range(PIECES):
            part = slice(p * step, (p + 1) * step)
            expd = jnp.exp(sd[part, :LANES] - top)
            ex[part, :] = expd
            norm_sum += jnp.sum(expd, axis=0, keepdims=True)
        inverse = 1.0 / norm_sum
        for p in range(PIECES):
            part = slice(p * step, (p + 1) * step)
            cat[part, :LANES] = (ex[part, :] * inverse).astype(bf16)
        turned = mul(kvt[...], cat[:, :LANES])
        stacked[g, pl.ds(start, LANES), :] = turned.T
        return carry

    def gather_heads(upper):
        first = HEAD_DIM if upper else 0
        lanes = slice(first, first + HEAD_DIM)
        for g in range(LOCAL):
            for h in range(0, SHARED, 2):
                left = stacked[g, h * both : (h + 1) * both, lanes]
                right = stacked[g, (h + 1) * both : (h + 2) * both, lanes]
                at = (g * SHARED + h) * HEAD_DIM
                halves[:, at : at + LANES] = jnp.concatenate([left, right], axis=1).astype(bf16)

    gr_copies = []
    for g in range(LOCAL):
        kv_arrived(kvb, 0, g)
        kvt[...] = kvb[g].astype(f32).T.astype(bf16)
        acc[g] = jnp.zeros((total, LANES), f32)
        lax.fori_loop(0, stack // LANES, functools.partial(backward_chunk, g), 0)
        gsend[g] = acc[g].astype(bf16)
        for k in range(1, GROUP):
            to = lax.rem(member + k, GROUP)
            copy = remote(
                gsend.at[g, pl.ds(to * rows, rows)], grecv.at[k, g],
                gr_send.at[g, k], gr_recv.at[g, k], {"ctx": base + to},
            )
            copy.start()
            gr_copies.append(copy)
    gather_heads(False)
    gq_send[...] = halves[theirs, :]
    pair_copies.append(pair_copy(3, gq_send, gq_all.at[core]))
    gq_all[core] = halves[mine, :]

    for g in range(LOCAL):
        kv_arrived(kvf, 1, g)
        kvt[...] = kvf[g].astype(f32).T.astype(bf16)
        lax.fori_loop(0, stack // LANES, functools.partial(forward_chunk, g), 0)
    gather_heads(True)
    mix_send[...] = halves[theirs, :]
    pair_copies.append(pair_copy(4, mix_send, mix_all.at[core]))
    mix_all[core] = halves[mine, :]
    pair_arrived(4, mix_all.at[other])
    made = xf[mine, :].astype(f32)
    for p in range(PAIR):
        made += mul(mix_all[p], wo[p * half : (p + 1) * half, :])
    of[...] = made.astype(bf16)

    def shift(at, src, dst, where, edge, arrive_edge):
        small = remote(
            src.at[pl.ds(0, mem)], dst.at[pl.ds(0, mem)],
            sec_send.at[at, 0], sec_recv.at[at, 0], {"section": where},
        )
        large = remote(
            src.at[pl.ds(mem, tokens)], dst.at[pl.ds(mem, tokens)],
            sec_send.at[at, 1], sec_recv.at[at, 1], {"section": where},
        )
        small.start()

        @pl.when(section != edge)
        def _():
            large.start()

        def finish():
            small.wait()

            @pl.when(section != edge)
            def _():
                large.wait_send()

            @pl.when(section != arrive_edge)
            def _():
                large.wait_recv()

        return finish

    finish_f = shift(0, of, outf_h, after, sections - 1, 0)

    for g in range(LOCAL):
        own = acc[g, pl.ds(member * rows, rows), :]
        cross = None
        for k in range(1, GROUP):
            source = lax.rem(member + GROUP - k, GROUP)
            place = grecv.at[k, g]
            remote(
                place, place, gr_send.at[g, k], gr_recv.at[g, k], {"ctx": base + source}
            ).wait_recv()
            value = grecv[k, g].astype(f32)
            if k % PAIR == 0:
                own = own + value
            else:
                cross = value if cross is None else cross + value
        gsum[core * LOCAL + g] = own
        gsum[other * LOCAL + g] = cross
    pair_arrived(3, gq_all.at[other])
    parts = [gsum[h, :, :HEAD_DIM] for h in range(KV_HEADS)]
    parts += [gsum[h, :, HEAD_DIM:] for h in range(KV_HEADS)]
    grad_kv = jnp.concatenate(parts, axis=1).astype(bf16)
    grad_normed = mul(grad_kv, wkv[...], NT)
    for p in range(PAIR):
        grad_normed += mul(gq_all[p], wq[:, p * half : (p + 1) * half], NT)
    values, scale = norm(xb[mine, :])
    plain = values * scale
    pushed = gain * grad_normed
    grad_in = cot[mine, :].astype(f32) + scale * (
        pushed - plain * jnp.mean(pushed * plain, axis=-1, keepdims=True)
    )
    ob[...] = grad_in.astype(bf16)
    finish_b = shift(1, ob, outb_h, before, 0, sections - 1)

    for copy in pair_copies + kv_copies + gr_copies:
        copy.wait_send()
    finish_f()
    finish_b()


def shards(fwd_in, bwd_saved, bwd_cot, new_tokens, loss_cot, gain, w_query, w_keyval, w_out):
    section_now = lax.axis_index("section")
    sections = lax.axis_size("section")
    rows, width = fwd_in.shape[1:]
    mem = rows - new_tokens.shape[0]
    both = PAIR * rows
    total = GROUP * rows
    stack = SHARED * both
    half = width // PAIR
    anywhere = pl.BlockSpec(memory_space=pl.ANY)
    block = jax.ShapeDtypeStruct((rows, width), bf16)
    vmem = pltpu.VMEM
    dma = pltpu.SemaphoreType.DMA
    arrived, returned = pl.pallas_call(
        functools.partial(kernel, sections, mem),
        out_shape=(block, block),
        in_specs=[anywhere] * 3 + [pl.BlockSpec(memory_space=pltpu.VMEM)] + [anywhere] * 3,
        out_specs=(anywhere, anywhere),
        scratch_shapes=[
            vmem((both, width), bf16), vmem((both, width), bf16), vmem((both, width), bf16),
            vmem(w_query.shape[1:], bf16), vmem(w_keyval.shape[1:], bf16), vmem(w_out.shape[1:], bf16),
            vmem((both, width), bf16),
            vmem((LOCAL, total, LANES), bf16), vmem((LOCAL, total, LANES), bf16),
            vmem((LANES, total), bf16),
            vmem((LOCAL, stack, LANES), bf16), vmem((LOCAL, stack, LANES), bf16),
            vmem((LOCAL, stack, LANES), bf16),
            vmem((total, LANES), jnp.int32),
            vmem((total, 2 * LANES), f32), vmem((total, LANES), f32), vmem((total, 2 * LANES), bf16),
            vmem((LOCAL, total, LANES), f32), vmem((LOCAL, total, LANES), bf16),
            vmem((GROUP, LOCAL, rows, LANES), bf16), vmem((KV_HEADS, rows, LANES), f32),
            vmem((LOCAL, stack, LANES), f32), vmem((both, half), bf16),
            vmem((rows, half), bf16), vmem((PAIR, rows, half), bf16),
            vmem((rows, half), bf16), vmem((PAIR, rows, half), bf16),
            vmem((rows, width), bf16), vmem((rows, width), bf16),
            dma((6,)), dma((5,)), dma((5,)),
            dma((2, LOCAL, CHIPS)), dma((2, LOCAL, CHIPS)),
            dma((LOCAL, GROUP)), dma((LOCAL, GROUP)),
            dma((2, 2)), dma((2, 2)),
        ],
        compiler_params=pltpu.CompilerParams(
            collective_id=0, has_side_effects=True, vmem_limit_bytes=60 * 1024 * 1024
        ),
    )(fwd_in[0], bwd_saved[0], bwd_cot[0], gain, w_query[0], w_keyval[0], w_out[0])
    head_rows = jnp.concatenate([arrived[:mem], new_tokens], axis=0)
    fwd_next = jnp.where(section_now == 0, head_rows, arrived)[None]
    tail_rows = jnp.concatenate([returned[:mem], loss_cot], axis=0)
    cot_next = jnp.where(section_now == sections - 1, tail_rows, returned)[None]
    return (fwd_next, cot_next)


def solution(mesh):
    return jax.shard_map(
        shards,
        mesh=mesh,
        in_specs=(
            P("section", "ctx", None),
            P("section", "ctx", None),
            P("section", "ctx", None),
            P("ctx", None),
            P("ctx", None),
            P("section", None),
            P("section", None, None),
            P("section", None, None),
            P("section", None, None),
        ),
        out_specs=(P("section", "ctx", None), P("section", "ctx", None)),
        check_vma=False,
    )
```

time: 228 us -> 72 us (0.32)
  matrix products: 127 us -> 0 us
  Pallas kernels: 0 us -> 67.4 us
  waiting for transfers between devices: 39.5 us -> 0 us
  local copies, waits for them, and re-layouts: 25.7 us -> 1.53 us
  other arithmetic: 20.6 us -> 2.09 us
  starting transfers between devices: 12.1 us -> 0 us
    dot_general x28 -> x0, matrix products: 104 us -> none  [the longest x4 31.3 us: one_head(): jnp.einsum('grk,grd->kd', dscores, q_head, preferred_element_type=jnp.flo...]
    pallas_call x0 -> x1, Pallas kernels: none -> 67.4 us  [shards(): pl.pallas_call(functools.partial(kernel, sections, mem), out_shape=(block...]
    ppermute x11 -> x0, waiting for transfers between devices: 39.5 us -> none  [the longest x9 27 us: swapped(): return lax.ppermute(block, axis, route)]
    sub x8 -> x0, matrix products: 23.1 us -> none  [head_probs(): expd = jnp.exp(scores - top)]
    ppermute x11 -> x0, starting transfers between devices: 12.1 us -> none  [the longest x9 10.6 us: swapped(): return lax.ppermute(block, axis, route)]
    reshape x5 -> x0, local copies, waits for them, and re-layouts: 10 us -> none  [the longest x2 3.57 us: split_heads(): query.reshape(rows_q, KV_HEADS, shared, HEAD_DIM).transpose(1, 2, 0, 3)]
    select_n x7 -> x0, other arithmetic: 9.08 us -> none  [the longest x6 7.64 us: collect_pairs(): jnp.where(upper == 0, jnp.concatenate([stacked, partner], axis=0), jnp.co...]
    slice x8 -> x2, local copies, waits for them, and re-layouts: 8.71 us -> 1.52 us  [the longest x1 0.76 us: shards(): head_rows = jnp.concatenate([arrived[:mem], new_tokens], axis=0)]
  transfers between devices with their start and end apart: 11 -> 0, of which waited for: 6 -> 0; matrix products, arithmetic and copies ran while one was open for 73% -> 0% of each run, Pallas kernels for 0% -> 0%
where the time goes in v1:
time: 72 us; the launch traced here: 71.7 us
  Pallas kernels  67.4 us (94%)
  other arithmetic  2.09 us (3%)
  local copies, waits for them, and re-layouts  1.53 us (2%)
    pallas_call x1, Pallas kernels, shards(): pl.pallas_call(functools.partial(kernel, sections, mem), out_shape=(block...  67.4 us
    broadcast_in_dim x1, other arithmetic, shards(): fwd_next = jnp.where(section_now == 0, head_rows, arrived)[None]  2.09 us

profile of v1, /device:TPU:11, one launch (start us, length us, event | category | flops | bytes accessed | tf_op | source)
XLA Modules:
  0.0 71.7 jit_solution(2360524307696583613)
XLA Ops:
  0.6 0.0 copy-start
  0.7 0.0 copy-start.1
  0.7 67.4 %shard_map.104 = (bf16[144,1024]{1,0:T(8,128)(2,1)}, bf16[144,1024]{1,0:T(8,128)(2,1)}) custom-call(bf16[144,1024]{1,0:T(8,128)(2,1)} %bitcast.13, bf16[144,1024]{1,0:T(8,128)(2,1)} %bitcast.14, bf16[144,1024]{1,0:T(8,128)(2,1)} %bitcast.15, bf16[1,1024]{1,0:T(2,128)(2,1)} %gain_ref.1, bf16[1024,1024]{1,0:T(8,128)(2,1)} %bitcast.10, ...), custom_call_target="tpu_custom_call" | custom-call | tf_op jit(solution)/shard_map/pallas_call | solution.py:387
  68.1 0.8 %slice.6 = bf16[16,1024]{1,0:T(8,128)(2,1)S(1)} slice(bf16[144,1024]{1,0:T(8,128)(2,1)} %get-tuple-element.4), slice={[0:16], [0:1024]} | slice | bytes 65536 | tf_op jit(solution)/shard_map/slice | solution.py:417
  68.8 0.8 %slice.7 = bf16[16,1024]{1,0:T(8,128)(2,1)S(1)} slice(bf16[144,1024]{1,0:T(8,128)(2,1)} %get-tuple-element.5), slice={[0:16], [0:1024]} | slice | bytes 65536 | tf_op jit(solution)/shard_map/slice | solution.py:419
  69.6 0.0 copy-done
  69.6 0.0 copy-done.1
  69.6 2.1 %fusion = (bf16[1,144,1024]{2,1,0:T(8,128)(2,1)}, bf16[1,144,1024]{2,1,0:T(8,128)(2,1)}) fusion(bf16[144,1024]{1,0:T(8,128)(2,1)} %get-tuple-element.4, bf16[128,1024]{1,0:T(8,128)(2,1)S(1)} %copy-done, bf16[16,1024]{1,0:T(8,128)(2,1)S(1)} %slice.6, pred[]{:T(512)S(6)} %eq.6, bf16[144,1024]{1,0:T(8,128)(2,1)} %get-tuple-element.5, ...), kind=kLoop, calls=%fused_computation.1 | loop fusion | flops 1474560 | bytes 1769474 | tf_op jit(solution)/shard_map/broadcast_in_dim | solution.py:418
Async XLA Ops:
  0.6 69.0 %copy-start = (bf16[128,1024]{1,0:T(8,128)(2,1)S(1)}, bf16[128,1024]{1,0:T(8,128)(2,1)}, u32[]{:S(2)}) copy-start(bf16[128,1024]{1,0:T(8,128)(2,1)} %param.12) | copy-start | bytes 786436
  0.7 69.0 %copy-start.1 = (bf16[128,1024]{1,0:T(8,128)(2,1)S(1)}, bf16[128,1024]{1,0:T(8,128)(2,1)}, u32[]{:S(2)}) copy-start(bf16[128,1024]{1,0:T(8,128)(2,1)} %param.13) | copy-start | bytes 786436

commit v2 on v1

--- a/solution.py
+++ b/solution.py
@@ -36,9 +36,10 @@
     xf_h, xb_h, cot_h, gain_ref, wq_h, wkv_h, wo_h,
     outf_h, outb_h,
     xf, xb, cot, wq, wkv, wo, normed, kvf, kvb, kvt, qf, qb, gb, kpos,
-    sd, ex, cat, acc, gsend, grecv, gsum, stacked, halves, gq_send, gq_all, mix_send, mix_all,
+    sd, ex, cat, acc, gsend, grecv, gpass, gsum, kvown, stacked, halves, gq_send, gq_all, mix_send, mix_all,
     of, ob,
     local_sem, pair_send, pair_recv, kv_send, kv_recv, gr_send, gr_recv, sec_send, sec_recv,
+    hop_send, hop_recv,
 ):
     rows = xf_h.shape[0]
     width = xf_h.shape[1]
@@ -47,7 +48,6 @@
     stack = SHARED * both
     half = width // PAIR
     tokens = rows - mem
-    kcols = LOCAL * HEAD_DIM
 
     ctx = lax.axis_index("ctx")
     section = lax.axis_index("section")
@@ -121,44 +121,156 @@
         scale = lax.rsqrt(jnp.mean(values * values, axis=-1, keepdims=True) + epsilon)
         return values, scale
 
-    def make_normed(x_ref):
-        for b in range(PAIR):
-            values, scale = norm(x_ref[b * rows : (b + 1) * rows, :])
-            normed[b * rows : (b + 1) * rows, :] = (values * scale * gain).astype(bf16)
-
-    chip_rows = pl.ds(chip * both, both)
+    def make_normed(x_ref, place):
+        values, scale = norm(x_ref[place, :])
+        normed[place, :] = (values * scale * gain).astype(bf16)
+
+    last = CHIPS - 1
+    is_end = jnp.logical_or(chip == 0, chip == last)
+    is_middle = jnp.logical_not(is_end)
+    opposite = last - chip
+    hop_from = jnp.where(chip == 1, last, 0)
+    hop_to = last - hop_from
+    sum_via = jnp.where(chip == 0, 1, last - 1)
+    sum_from = jnp.where(chip == 1, 0, last)
+
+    def peer(k):
+        return lax.rem(member + k, GROUP)
+
+    def source(k):
+        return lax.rem(member + GROUP - k, GROUP)
+
+    def is_far(one):
+        return jnp.logical_and(is_end, one // PAIR == opposite)
+
+    order = sorted(range(1, GROUP), key=lambda k: abs(k - GROUP // 2))
 
     def project_kv(kv_ref, kind):
-        keys = mul(normed[...], wkv[:, pl.ds(pl.multiple_of(core * kcols, kcols), kcols)])
-        vals = mul(
-            normed[...],
-            wkv[:, pl.ds(pl.multiple_of(KV_HEADS * HEAD_DIM + core * kcols, kcols), kcols)],
-        )
+        keyval = mul(normed[mine, :], wkv[...])
+        for h in range(KV_HEADS):
+            at = h * HEAD_DIM
+            after_keys = KV_HEADS * HEAD_DIM + at
+            kvown[kind, h] = jnp.concatenate(
+                [keyval[:, at : at + HEAD_DIM], keyval[:, after_keys : after_keys + HEAD_DIM]],
+                axis=1,
+            ).astype(bf16)
         for g in range(LOCAL):
-            lanes = slice(g * HEAD_DIM, (g + 1) * HEAD_DIM)
-            kv_ref[g, chip_rows, :] = jnp.concatenate(
-                [keys[:, lanes], vals[:, lanes]], axis=1
-            ).astype(bf16)
-        copies = []
+            kv_ref[g, pl.ds(member * rows, rows), :] = kvown[kind, core * LOCAL + g]
+
+    def kv_copy(kv_ref, kind, g, k):
+        to = peer(k)
+        return remote(
+            kvown.at[kind, lax.rem(to, PAIR) * LOCAL + g],
+            kv_ref.at[g, pl.ds(member * rows, rows)],
+            kv_send.at[kind, g, k], kv_recv.at[kind, g, k], {"ctx": base + to},
+        )
+
+    def send_kv(kv_ref, kind):
         for g in range(LOCAL):
-            for k in range(1, CHIPS):
-                to = base + lax.rem(chip + k, CHIPS) * PAIR + core
-                copy = remote(
-                    kv_ref.at[g, chip_rows], kv_ref.at[g, chip_rows],
-                    kv_send.at[kind, g, k], kv_recv.at[kind, g, k], {"ctx": to},
-                )
-                copy.start()
-                copies.append(copy)
-        return copies
+            for k in order:
+                @pl.when(jnp.logical_not(is_far(peer(k))))
+                def _():
+                    kv_copy(kv_ref, kind, g, k).start()
+
+    def finish_kv(kv_ref, kind):
+        for g in range(LOCAL):
+            for k in order:
+                @pl.when(jnp.logical_not(is_far(peer(k))))
+                def _():
+                    kv_copy(kv_ref, kind, g, k).wait_send()
+
+            @pl.when(is_middle)
+            def _():
+                hop_copy(kv_ref, kind, g).wait_send()
+
+    def hop_copy(kv_ref, kind, g):
+        place = kv_ref.at[g, pl.ds(hop_from * both, both)]
+        return remote(
+            place, place, hop_send.at[kind, g], hop_recv.at[kind, g],
+            {"ctx": base + hop_to * PAIR + core},
+        )
+
+    def kv_wait(kv_ref, kind, g, one):
+        k = lax.rem(member + GROUP - one, GROUP)
+        place = kv_ref.at[g, pl.ds(one * rows, rows)]
+        remote(
+            place, place, kv_send.at[kind, g, k], kv_recv.at[kind, g, k], {"ctx": base + one}
+        ).wait_recv()
+
+    def hop_kv(kv_ref, kind, g):
+        @pl.when(is_middle)
+        def _():
+            for c in range(PAIR):
+                kv_wait(kv_ref, kind, g, hop_from * PAIR + c)
+            hop_copy(kv_ref, kind, g).start()
 
     def kv_arrived(kv_ref, kind, g):
-        for k in range(1, CHIPS):
-            source = lax.rem(chip + CHIPS - k, CHIPS)
-            place = kv_ref.at[g, pl.ds(source * both, both)]
+        for k in range(1, GROUP):
+            one = source(k)
+            done = jnp.logical_and(is_middle, one // PAIR == hop_from)
+
+            @pl.when(jnp.logical_not(jnp.logical_or(is_far(one), done)))
+            def _():
+                kv_wait(kv_ref, kind, g, one)
+
+        @pl.when(is_end)
+        def _():
+            place = kv_ref.at[g, pl.ds(opposite * both, both)]
             remote(
-                place, place, kv_send.at[kind, g, k], kv_recv.at[kind, g, k],
-                {"ctx": base + source * PAIR + core},
+                place, place, hop_send.at[kind, g], hop_recv.at[kind, g],
+                {"ctx": base + opposite * PAIR + core},
             ).wait_recv()
+
+    def gr_copy(g, k):
+        to = peer(k)
+        return remote(
+            gsend.at[g, pl.ds(to * rows, rows)], grecv.at[k, g],
+            gr_send.at[g, k], gr_recv.at[g, k], {"ctx": base + to},
+        )
+
+    def is_summed(one):
+        return jnp.logical_and(is_middle, one // PAIR == last - sum_from)
+
+    def sum_copy(g, where):
+        return remote(
+            gsend.at[g, pl.ds(opposite * both, both)], gpass.at[g],
+            hop_send.at[2, g], hop_recv.at[2, g], {"ctx": base + where * PAIR + core},
+        )
+
+    def send_sums(g):
+        gsend[g] = acc[g].astype(bf16)
+
+        @pl.when(is_end)
+        def _():
+            sum_copy(g, sum_via).start()
+
+        for k in order:
+            to = peer(k)
+
+            @pl.when(jnp.logical_not(jnp.logical_or(is_far(to), is_summed(to))))
+            def _():
+                gr_copy(g, k).start()
+
+    def hop_sums(g):
+        @pl.when(is_middle)
+        def _():
+            sum_copy(g, sum_from).wait_recv()
+            place = pl.ds((last - sum_from) * both, both)
+            gsend[g, place, :] = (acc[g, place, :] + gpass[g].astype(f32)).astype(bf16)
+            for k in order:
+                @pl.when(is_summed(peer(k)))
+                def _():
+                    gr_copy(g, k).start()
+
+    def finish_sums(g):
+        @pl.when(is_end)
+        def _():
+            sum_copy(g, sum_via).wait_send()
+
+        for k in order:
+            @pl.when(jnp.logical_not(is_far(peer(k))))
+            def _():
+                gr_copy(g, k).wait_send()
 
     def spread(matrix, dst, upper, factor):
         rounded = matrix.astype(bf16).astype(f32) * factor
@@ -174,20 +286,24 @@
     my_cols = pl.ds(pl.multiple_of(core * half, half), half)
 
     load_xb.wait()
+    make_normed(xb, mine)
+    load_wkv.wait()
+    project_kv(kvb, 0)
+    send_kv(kvb, 0)
     pair_arrived(0, xb.at[theirs])
-    make_normed(xb)
-    load_wkv.wait()
-    kv_copies = project_kv(kvb, 0)
+    make_normed(xb, theirs)
     load_wq.wait()
     spread(mul(normed[...], wq[:, my_cols]), qb, False, scale_by)
-    load_xf.wait()
-    pair_arrived(1, xf.at[theirs])
-    make_normed(xf)
-    kv_copies += project_kv(kvf, 1)
     load_cot.wait()
     pair_arrived(2, cot.at[theirs])
     load_wo.wait()
     spread(mul(cot[...], wo[my_cols, :], NT), gb, True, 1.0)
+    load_xf.wait()
+    make_normed(xf, mine)
+    project_kv(kvf, 1)
+    hop_kv(kvb, 0, 0)
+    pair_arrived(1, xf.at[theirs])
+    make_normed(xf, theirs)
     spread(mul(normed[...], wq[:, my_cols]), qf, False, scale_by)
 
     step = total // PIECES
@@ -269,21 +385,28 @@
                 at = (g * SHARED + h) * HEAD_DIM
                 halves[:, at : at + LANES] = jnp.concatenate([left, right], axis=1).astype(bf16)
 
-    gr_copies = []
+    def run(chunk, g, actions):
+        def body(i, carry):
+            for at, action in actions.items():
+                pl.when(i == at)(action)
+            return chunk(g, i, carry)
+
+        lax.fori_loop(0, stack // LANES, body, 0)
+
+    def go_on():
+        hop_kv(kvb, 0, 1)
+        send_kv(kvf, 1)
+
+    backward_actions = [
+        {2: go_on},
+        {1: lambda: hop_kv(kvf, 1, 0), 4: lambda: hop_sums(0), 7: lambda: hop_kv(kvf, 1, 1)},
+    ]
     for g in range(LOCAL):
         kv_arrived(kvb, 0, g)
         kvt[...] = kvb[g].astype(f32).T.astype(bf16)
         acc[g] = jnp.zeros((total, LANES), f32)
-        lax.fori_loop(0, stack // LANES, functools.partial(backward_chunk, g), 0)
-        gsend[g] = acc[g].astype(bf16)
-        for k in range(1, GROUP):
-            to = lax.rem(member + k, GROUP)
-            copy = remote(
-                gsend.at[g, pl.ds(to * rows, rows)], grecv.at[k, g],
-                gr_send.at[g, k], gr_recv.at[g, k], {"ctx": base + to},
-            )
-            copy.start()
-            gr_copies.append(copy)
+        run(backward_chunk, g, backward_actions[g])
+        send_sums(g)
     gather_heads(False)
     gq_send[...] = halves[theirs, :]
     pair_copies.append(pair_copy(3, gq_send, gq_all.at[core]))
@@ -292,7 +415,7 @@
     for g in range(LOCAL):
         kv_arrived(kvf, 1, g)
         kvt[...] = kvf[g].astype(f32).T.astype(bf16)
-        lax.fori_loop(0, stack // LANES, functools.partial(forward_chunk, g), 0)
+        run(forward_chunk, g, {3: lambda: hop_sums(1)} if g == 0 else {})
     gather_heads(True)
     mix_send[...] = halves[theirs, :]
     pair_copies.append(pair_copy(4, mix_send, mix_all.at[core]))
@@ -337,11 +460,19 @@
         own = acc[g, pl.ds(member * rows, rows), :]
         cross = None
         for k in range(1, GROUP):
-            source = lax.rem(member + GROUP - k, GROUP)
-            place = grecv.at[k, g]
-            remote(
-                place, place, gr_send.at[g, k], gr_recv.at[g, k], {"ctx": base + source}
-            ).wait_recv()
+            one = source(k)
+
+            @pl.when(is_far(one))
+            def _():
+                grecv[k, g] = jnp.zeros((rows, LANES), bf16)
+
+            @pl.when(jnp.logical_not(is_far(one)))
+            def _():
+                place = grecv.at[k, g]
+                remote(
+                    place, place, gr_send.at[g, k], gr_recv.at[g, k], {"ctx": base + one}
+                ).wait_recv()
+
             value = grecv[k, g].astype(f32)
             if k % PAIR == 0:
                 own = own + value
@@ -365,8 +496,12 @@
     ob[...] = grad_in.astype(bf16)
     finish_b = shift(1, ob, outb_h, before, 0, sections - 1)
 
-    for copy in pair_copies + kv_copies + gr_copies:
+    for copy in pair_copies:
         copy.wait_send()
+    finish_kv(kvb, 0)
+    finish_kv(kvf, 1)
+    for g in range(LOCAL):
+        finish_sums(g)
     finish_f()
     finish_b()
 
@@ -400,24 +535,27 @@
             vmem((total, LANES), jnp.int32),
             vmem((total, 2 * LANES), f32), vmem((total, LANES), f32), vmem((total, 2 * LANES), bf16),
             vmem((LOCAL, total, LANES), f32), vmem((LOCAL, total, LANES), bf16),
-            vmem((GROUP, LOCAL, rows, LANES), bf16), vmem((KV_HEADS, rows, LANES), f32),
+            vmem((GROUP, LOCAL, rows, LANES), bf16), vmem((LOCAL, both, LANES), bf16),
+            vmem((KV_HEADS, rows, LANES), f32), vmem((2, KV_HEADS, rows, LANES), bf16),
             vmem((LOCAL, stack, LANES), f32), vmem((both, half), bf16),
             vmem((rows, half), bf16), vmem((PAIR, rows, half), bf16),
             vmem((rows, half), bf16), vmem((PAIR, rows, half), bf16),
             vmem((rows, width), bf16), vmem((rows, width), bf16),
             dma((6,)), dma((5,)), dma((5,)),
-            dma((2, LOCAL, CHIPS)), dma((2, LOCAL, CHIPS)),
+            dma((2, LOCAL, GROUP)), dma((2, LOCAL, GROUP)),
             dma((LOCAL, GROUP)), dma((LOCAL, GROUP)),
             dma((2, 2)), dma((2, 2)),
+            dma((3, LOCAL)), dma((3, LOCAL)),
         ],
         compiler_params=pltpu.CompilerParams(
             collective_id=0, has_side_effects=True, vmem_limit_bytes=60 * 1024 * 1024
         ),
     )(fwd_in[0], bwd_saved[0], bwd_cot[0], gain, w_query[0], w_keyval[0], w_out[0])
-    head_rows = jnp.concatenate([arrived[:mem], new_tokens], axis=0)
-    fwd_next = jnp.where(section_now == 0, head_rows, arrived)[None]
-    tail_rows = jnp.concatenate([returned[:mem], loss_cot], axis=0)
-    cot_next = jnp.where(section_now == sections - 1, tail_rows, returned)[None]
+    token_row = lax.broadcasted_iota(jnp.int32, (rows, 1), 0) >= mem
+    edge = jnp.pad(new_tokens, ((mem, 0), (0, 0)))
+    fwd_next = jnp.where(token_row & (section_now == 0), edge, arrived)[None]
+    edge = jnp.pad(loss_cot, ((mem, 0), (0, 0)))
+    cot_next = jnp.where(token_row & (section_now == sections - 1), edge, returned)[None]
     return (fwd_next, cot_next)
 
 

time: 72 us -> 69.7 us (0.968); the launches traced: 71.7 us -> 68.4 us
  Pallas kernels: 67.4 us -> 65.6 us
  local copies, waits for them, and re-layouts: 1.53 us -> 0.01 us
    pallas_call x1, Pallas kernels: 67.4 us -> 65.6 us  [shards(): pl.pallas_call(functools.partial(kernel, sections, mem), out_shape=(block...]
    slice x2 -> x0, local copies, waits for them, and re-layouts: 1.52 us -> none  [the longest x1 0.76 us: shards(): head_rows = jnp.concatenate([arrived[:mem], new_tokens], axis=0)]
where the time goes in v2:
time: 69.7 us; the launch traced here: 68.4 us
  Pallas kernels  65.6 us (94%)
  other arithmetic  2.09 us (3%)
    pallas_call x1, Pallas kernels, shards(): pl.pallas_call(functools.partial(kernel, sections, mem), out_shape=(block...  65.6 us
    broadcast_in_dim x1, other arithmetic, shards(): jnp.where(token_row & (section_now == sections - 1), edge, returned)[None]  2.07 us

profile of v2, /device:TPU:11, one launch (start us, length us, event | category | flops | bytes accessed | tf_op | source)
XLA Modules:
  0.0 68.4 jit_solution(8126632761990086914)
XLA Ops:
  0.7 0.0 copy-start
  0.7 0.0 copy-start.1
  0.7 65.6 %shard_map.104 = (bf16[144,1024]{1,0:T(8,128)(2,1)}, bf16[144,1024]{1,0:T(8,128)(2,1)}) custom-call(bf16[144,1024]{1,0:T(8,128)(2,1)} %bitcast.13, bf16[144,1024]{1,0:T(8,128)(2,1)} %bitcast.14, bf16[144,1024]{1,0:T(8,128)(2,1)} %bitcast.15, bf16[1,1024]{1,0:T(2,128)(2,1)} %gain_ref.1, bf16[1024,1024]{1,0:T(8,128)(2,1)} %bitcast.10, ...), custom_call_target="tpu_custom_call" | custom-call | tf_op jit(solution)/shard_map/pallas_call | solution.py:522
  66.3 0.0 copy-done
  66.3 0.0 copy-done.1
  66.3 2.1 %select_bitcast_fusion = (bf16[1,144,1024]{2,1,0:T(8,128)(2,1)}, bf16[1,144,1024]{2,1,0:T(8,128)(2,1)}) fusion(bf16[144,1024]{1,0:T(8,128)(2,1)} %get-tuple-element.5, bf16[128,1024]{1,0:T(8,128)(2,1)S(1)} %copy-done, pred[144]{0:T(512)(128)(4,1)S(1)} %fusion, bf16[144,1024]{1,0:T(8,128)(2,1)} %get-tuple-element.4, bf16[128,1024]{1,0:T(8,128)(2,1)S(1)} %copy-done.1, ...), kind=kLoop, calls=%fused_computation | loop fusion | flops 294912 | bytes 1704224 | tf_op jit(solution)/shard_map/broadcast_in_dim | solution.py:558
  (2 shorter events, 0.0 us)
Async XLA Ops:
  0.7 65.6 %copy-start = (bf16[128,1024]{1,0:T(8,128)(2,1)S(1)}, bf16[128,1024]{1,0:T(8,128)(2,1)}, u32[]{:S(2)}) copy-start(bf16[128,1024]{1,0:T(8,128)(2,1)} %param.13) | copy-start | bytes 786436
  0.7 65.6 %copy-start.1 = (bf16[128,1024]{1,0:T(8,128)(2,1)S(1)}, bf16[128,1024]{1,0:T(8,128)(2,1)}, u32[]{:S(2)}) copy-start(bf16[128,1024]{1,0:T(8,128)(2,1)} %param.12) | copy-start | bytes 786436

commit v3 on v2

--- a/solution.py
+++ b/solution.py
@@ -17,6 +17,7 @@
 SHARED = HEADS // KV_HEADS
 LANES = 128
 PIECES = 4
+UNROLL = 3
 
 epsilon = 1e-05
 far = 1 << 30
@@ -316,64 +317,70 @@
         inner = row - block * rows
         return jnp.where(inner < mem, far, (chip * PAIR + block) * tokens + inner - mem)
 
-    def backward_chunk(g, i, carry):
-        start = pl.multiple_of(i * LANES, LANES)
-        pair = jnp.concatenate([qb[g, pl.ds(start, LANES), :], gb[g, pl.ds(start, LANES), :]], axis=0)
-        position = query_positions(start)
-        top = None
-        for p in range(PIECES):
-            part = slice(p * step, (p + 1) * step)
-            product = mul(kvb[g, part, :], pair, NT)
-            scores = jnp.where(kpos[part, :] <= position, product[:, :LANES], -1e30)
-            sd[part, :LANES] = scores
-            sd[part, LANES:] = product[:, LANES:]
-            peak = jnp.max(scores, axis=0, keepdims=True)
-            top = peak if top is None else jnp.maximum(top, peak)
-        norm_sum = jnp.zeros((1, LANES), f32)
-        delta = jnp.zeros((1, LANES), f32)
-        for p in range(PIECES):
-            part = slice(p * step, (p + 1) * step)
-            expd = jnp.exp(sd[part, :LANES] - top)
-            ex[part, :] = expd
-            norm_sum += jnp.sum(expd, axis=0, keepdims=True)
-            delta += jnp.sum(expd * sd[part, LANES:], axis=0, keepdims=True)
-        inverse = 1.0 / norm_sum
-        delta = delta * inverse
-        for p in range(PIECES):
-            part = slice(p * step, (p + 1) * step)
-            probs = ex[part, :] * inverse
-            cat[part, LANES:] = probs.astype(bf16)
-            cat[part, :LANES] = (probs * (sd[part, LANES:] - delta)).astype(bf16)
-            acc[g, part, :] += mul(cat[part, :], pair)
-        turned = mul(kvt[...], cat[:, :LANES])
-        stacked[g, pl.ds(start, LANES), :] = turned.T * scale_by
-        return carry
-
-    def forward_chunk(g, i, carry):
-        start = pl.multiple_of(i * LANES, LANES)
-        queries = qf[g, pl.ds(start, LANES), :]
-        position = query_positions(start)
-        top = None
-        for p in range(PIECES):
-            part = slice(p * step, (p + 1) * step)
-            product = mul(kvf[g, part, :], queries, NT)
-            scores = jnp.where(kpos[part, :] <= position, product, -1e30)
-            sd[part, :LANES] = scores
-            peak = jnp.max(scores, axis=0, keepdims=True)
-            top = peak if top is None else jnp.maximum(top, peak)
-        norm_sum = jnp.zeros((1, LANES), f32)
-        for p in range(PIECES):
-            part = slice(p * step, (p + 1) * step)
-            expd = jnp.exp(sd[part, :LANES] - top)
-            ex[part, :] = expd
-            norm_sum += jnp.sum(expd, axis=0, keepdims=True)
-        inverse = 1.0 / norm_sum
-        for p in range(PIECES):
-            part = slice(p * step, (p + 1) * step)
-            cat[part, :LANES] = (ex[part, :] * inverse).astype(bf16)
-        turned = mul(kvt[...], cat[:, :LANES])
-        stacked[g, pl.ds(start, LANES), :] = turned.T
-        return carry
+    parts = [slice(p * step, (p + 1) * step) for p in range(PIECES)]
+
+    def backward_chunk(g, chunks):
+        starts = [pl.multiple_of(i * LANES, LANES) for i in chunks]
+        pairs = [
+            jnp.concatenate([qb[g, pl.ds(at, LANES), :], gb[g, pl.ds(at, LANES), :]], axis=0)
+            for at in starts
+        ]
+        for u, start in enumerate(starts):
+            position = query_positions(start)
+            top = None
+            for part in parts:
+                product = mul(kvb[g, part, :], pairs[u], NT)
+                scores = jnp.where(kpos[part, :] <= position, product[:, :LANES], -1e30)
+                sd[u, part, :LANES] = scores
+                sd[u, part, LANES:] = product[:, LANES:]
+                peak = jnp.max(scores, axis=0, keepdims=True)
+                top = peak if top is None else jnp.maximum(top, peak)
+            norm_sum = jnp.zeros((1, LANES), f32)
+            delta = jnp.zeros((1, LANES), f32)
+            for part in parts:
+                expd = jnp.exp(sd[u, part, :LANES] - top)
+                ex[u, part, :] = expd
+                norm_sum += jnp.sum(expd, axis=0, keepdims=True)
+                delta += jnp.sum(expd * sd[u, part, LANES:], axis=0, keepdims=True)
+            inverse = 1.0 / norm_sum
+            delta = delta * inverse
+            at = u * 2 * LANES
+            for part in parts:
+                probs = ex[u, part, :] * inverse
+                cat[part, at + LANES : at + 2 * LANES] = probs.astype(bf16)
+                cat[part, at : at + LANES] = (probs * (sd[u, part, LANES:] - delta)).astype(bf16)
+        everything = jnp.concatenate(pairs, axis=0)
+        for part in parts:
+            acc[g, part, :] += mul(cat[part, :], everything)
+        for u, start in enumerate(starts):
+            at = u * 2 * LANES
+            turned = mul(kvt[...], cat[:, at : at + LANES])
+            stacked[g, pl.ds(start, LANES), :] = turned.T * scale_by
+
+    def forward_chunk(g, chunks):
+        for u, i in enumerate(chunks):
+            start = pl.multiple_of(i * LANES, LANES)
+            queries = qf[g, pl.ds(start, LANES), :]
+            position = query_positions(start)
+            top = None
+            for part in parts:
+                product = mul(kvf[g, part, :], queries, NT)
+                scores = jnp.where(kpos[part, :] <= position, product, -1e30)
+                sd[u, part, :LANES] = scores
+                peak = jnp.max(scores, axis=0, keepdims=True)
+                top = peak if top is None else jnp.maximum(top, peak)
+            norm_sum = jnp.zeros((1, LANES), f32)
+            for part in parts:
+                expd = jnp.exp(sd[u, part, :LANES] - top)
+                ex[u, part, :] = expd
+                norm_sum += jnp.sum(expd, axis=0, keepdims=True)
+            inverse = 1.0 / norm_sum
+            for part in parts:
+                cat[part, u * LANES : (u + 1) * LANES] = (ex[u, part, :] * inverse).astype(bf16)
+        turned = mul(kvt[...], cat[:, : len(chunks) * LANES])
+        for u, i in enumerate(chunks):
+            start = pl.multiple_of(i * LANES, LANES)
+            stacked[g, pl.ds(start, LANES), :] = turned[:, u * LANES : (u + 1) * LANES].T
 
     def gather_heads(upper):
         first = HEAD_DIM if upper else 0
@@ -389,17 +396,22 @@
         def body(i, carry):
             for at, action in actions.items():
                 pl.when(i == at)(action)
-            return chunk(g, i, carry)
-
-        lax.fori_loop(0, stack // LANES, body, 0)
+            chunk(g, [i * UNROLL + u for u in range(UNROLL)])
+            return carry
+
+        lax.fori_loop(0, stack // LANES // UNROLL, body, 0)
 
     def go_on():
         hop_kv(kvb, 0, 1)
         send_kv(kvf, 1)
 
+    def late():
+        hop_sums(0)
+        hop_kv(kvf, 1, 1)
+
     backward_actions = [
-        {2: go_on},
-        {1: lambda: hop_kv(kvf, 1, 0), 4: lambda: hop_sums(0), 7: lambda: hop_kv(kvf, 1, 1)},
+        {1: go_on},
+        {1: lambda: hop_kv(kvf, 1, 0), 2: late},
     ]
     for g in range(LOCAL):
         kv_arrived(kvb, 0, g)
@@ -415,7 +427,7 @@
     for g in range(LOCAL):
         kv_arrived(kvf, 1, g)
         kvt[...] = kvf[g].astype(f32).T.astype(bf16)
-        run(forward_chunk, g, {3: lambda: hop_sums(1)} if g == 0 else {})
+        run(forward_chunk, g, {2: lambda: hop_sums(1)} if g == 0 else {})
     gather_heads(True)
     mix_send[...] = halves[theirs, :]
     pair_copies.append(pair_copy(4, mix_send, mix_all.at[core]))
@@ -481,9 +493,9 @@
         gsum[core * LOCAL + g] = own
         gsum[other * LOCAL + g] = cross
     pair_arrived(3, gq_all.at[other])
-    parts = [gsum[h, :, :HEAD_DIM] for h in range(KV_HEADS)]
-    parts += [gsum[h, :, HEAD_DIM:] for h in range(KV_HEADS)]
-    grad_kv = jnp.concatenate(parts, axis=1).astype(bf16)
+    columns = [gsum[h, :, :HEAD_DIM] for h in range(KV_HEADS)]
+    columns += [gsum[h, :, HEAD_DIM:] for h in range(KV_HEADS)]
+    grad_kv = jnp.concatenate(columns, axis=1).astype(bf16)
     grad_normed = mul(grad_kv, wkv[...], NT)
     for p in range(PAIR):
         grad_normed += mul(gq_all[p], wq[:, p * half : (p + 1) * half], NT)
@@ -533,7 +545,8 @@
             vmem((LOCAL, stack, LANES), bf16), vmem((LOCAL, stack, LANES), bf16),
             vmem((LOCAL, stack, LANES), bf16),
             vmem((total, LANES), jnp.int32),
-            vmem((total, 2 * LANES), f32), vmem((total, LANES), f32), vmem((total, 2 * LANES), bf16),
+            vmem((UNROLL, total, 2 * LANES), f32), vmem((UNROLL, total, LANES), f32),
+            vmem((total, UNROLL * 2 * LANES), bf16),
             vmem((LOCAL, total, LANES), f32), vmem((LOCAL, total, LANES), bf16),
             vmem((GROUP, LOCAL, rows, LANES), bf16), vmem((LOCAL, both, LANES), bf16),
             vmem((KV_HEADS, rows, LANES), f32), vmem((2, KV_HEADS, rows, LANES), bf16),

time: 69.7 us -> 56.8 us (0.81)
  Pallas kernels: 65.6 us -> 53 us
    pallas_call x1, Pallas kernels: 65.6 us -> 53 us  [shards(): pl.pallas_call(functools.partial(kernel, sections, mem), out_shape=(block...]
where the time goes in v3:
time: 56.8 us; the launch traced here: 55.7 us
  Pallas kernels  53 us (93%)
  other arithmetic  2.09 us (4%)
  between operations  0.69 us (1%)
    pallas_call x1, Pallas kernels, shards(): pl.pallas_call(functools.partial(kernel, sections, mem), out_shape=(block...  53 us
    broadcast_in_dim x1, other arithmetic, shards(): jnp.where(token_row & (section_now == sections - 1), edge, returned)[None]  2.07 us

profile of v3, /device:TPU:11, one launch (start us, length us, event | category | flops | bytes accessed | tf_op | source)
XLA Modules:
  0.0 55.7 jit_solution(2137623879940189096)
XLA Ops:
  0.7 0.0 copy-start
  0.7 0.0 copy-start.1
  0.7 53.0 %shard_map.104 = (bf16[144,1024]{1,0:T(8,128)(2,1)}, bf16[144,1024]{1,0:T(8,128)(2,1)}) custom-call(bf16[144,1024]{1,0:T(8,128)(2,1)} %bitcast.13, bf16[144,1024]{1,0:T(8,128)(2,1)} %bitcast.14, bf16[144,1024]{1,0:T(8,128)(2,1)} %bitcast.15, bf16[1,1024]{1,0:T(2,128)(2,1)} %gain_ref.1, bf16[1024,1024]{1,0:T(8,128)(2,1)} %bitcast.10, ...), custom_call_target="tpu_custom_call" | custom-call | tf_op jit(solution)/shard_map/pallas_call | solution.py:534
  53.7 0.0 copy-done
  53.7 0.0 copy-done.1
  53.7 2.1 %select_bitcast_fusion = (bf16[1,144,1024]{2,1,0:T(8,128)(2,1)}, bf16[1,144,1024]{2,1,0:T(8,128)(2,1)}) fusion(bf16[144,1024]{1,0:T(8,128)(2,1)} %get-tuple-element.5, bf16[128,1024]{1,0:T(8,128)(2,1)S(1)} %copy-done, pred[144]{0:T(512)(128)(4,1)S(1)} %fusion, bf16[144,1024]{1,0:T(8,128)(2,1)} %get-tuple-element.4, bf16[128,1024]{1,0:T(8,128)(2,1)S(1)} %copy-done.1, ...), kind=kLoop, calls=%fused_computation | loop fusion | flops 294912 | bytes 1704224 | tf_op jit(solution)/shard_map/broadcast_in_dim | solution.py:571
  (2 shorter events, 0.0 us)
Async XLA Ops:
  0.7 53.0 %copy-start = (bf16[128,1024]{1,0:T(8,128)(2,1)S(1)}, bf16[128,1024]{1,0:T(8,128)(2,1)}, u32[]{:S(2)}) copy-start(bf16[128,1024]{1,0:T(8,128)(2,1)} %param.13) | copy-start | bytes 786436
  0.7 53.0 %copy-start.1 = (bf16[128,1024]{1,0:T(8,128)(2,1)S(1)}, bf16[128,1024]{1,0:T(8,128)(2,1)}, u32[]{:S(2)}) copy-start(bf16[128,1024]{1,0:T(8,128)(2,1)} %param.12) | copy-start | bytes 786436

commit v4 on v3

--- a/solution.py
+++ b/solution.py
@@ -467,6 +467,12 @@
         return finish
 
     finish_f = shift(0, of, outf_h, after, sections - 1, 0)
+    pair_arrived(3, gq_all.at[other])
+    from_queries = mul(gq_all[0], wq[:, :half], NT)
+    for p in range(1, PAIR):
+        from_queries += mul(gq_all[p], wq[:, p * half : (p + 1) * half], NT)
+    values, scale = norm(xb[mine, :])
+    plain = values * scale
 
     for g in range(LOCAL):
         own = acc[g, pl.ds(member * rows, rows), :]
@@ -492,15 +498,10 @@
                 cross = value if cross is None else cross + value
         gsum[core * LOCAL + g] = own
         gsum[other * LOCAL + g] = cross
-    pair_arrived(3, gq_all.at[other])
     columns = [gsum[h, :, :HEAD_DIM] for h in range(KV_HEADS)]
     columns += [gsum[h, :, HEAD_DIM:] for h in range(KV_HEADS)]
     grad_kv = jnp.concatenate(columns, axis=1).astype(bf16)
-    grad_normed = mul(grad_kv, wkv[...], NT)
-    for p in range(PAIR):
-        grad_normed += mul(gq_all[p], wq[:, p * half : (p + 1) * half], NT)
-    values, scale = norm(xb[mine, :])
-    plain = values * scale
+    grad_normed = from_queries + mul(grad_kv, wkv[...], NT)
     pushed = gain * grad_normed
     grad_in = cot[mine, :].astype(f32) + scale * (
         pushed - plain * jnp.mean(pushed * plain, axis=-1, keepdims=True)

time: 56.8 us -> 56.8 us (level)
  no operation moved by 1% of the time
where the time goes in v4:
time: 56.8 us; the launch traced here: 55.7 us
  Pallas kernels  52.9 us (93%)
  other arithmetic  2.09 us (4%)
  between operations  0.69 us (1%)
    pallas_call x1, Pallas kernels, shards(): pl.pallas_call(functools.partial(kernel, sections, mem), out_shape=(block...  52.9 us
    broadcast_in_dim x1, other arithmetic, shards(): jnp.where(token_row & (section_now == sections - 1), edge, returned)[None]  2.07 us

profile of v4, /device:TPU:11, one launch (start us, length us, event | category | flops | bytes accessed | tf_op | source)
XLA Modules:
  0.0 55.7 jit_solution(8512139483064693727)
XLA Ops:
  0.7 0.0 copy-start
  0.7 0.0 copy-start.1
  0.7 52.9 %shard_map.104 = (bf16[144,1024]{1,0:T(8,128)(2,1)}, bf16[144,1024]{1,0:T(8,128)(2,1)}) custom-call(bf16[144,1024]{1,0:T(8,128)(2,1)} %bitcast.13, bf16[144,1024]{1,0:T(8,128)(2,1)} %bitcast.14, bf16[144,1024]{1,0:T(8,128)(2,1)} %bitcast.15, bf16[1,1024]{1,0:T(2,128)(2,1)} %gain_ref.1, bf16[1024,1024]{1,0:T(8,128)(2,1)} %bitcast.10, ...), custom_call_target="tpu_custom_call" | custom-call | tf_op jit(solution)/shard_map/pallas_call | solution.py:535
  53.6 0.0 copy-done
  53.6 0.0 copy-done.1
  53.6 2.1 %select_bitcast_fusion = (bf16[1,144,1024]{2,1,0:T(8,128)(2,1)}, bf16[1,144,1024]{2,1,0:T(8,128)(2,1)}) fusion(bf16[144,1024]{1,0:T(8,128)(2,1)} %get-tuple-element.5, bf16[128,1024]{1,0:T(8,128)(2,1)S(1)} %copy-done, pred[144]{0:T(512)(128)(4,1)S(1)} %fusion, bf16[144,1024]{1,0:T(8,128)(2,1)} %get-tuple-element.4, bf16[128,1024]{1,0:T(8,128)(2,1)S(1)} %copy-done.1, ...), kind=kLoop, calls=%fused_computation | loop fusion | flops 294912 | bytes 1704224 | tf_op jit(solution)/shard_map/broadcast_in_dim | solution.py:572
  (2 shorter events, 0.0 us)
Async XLA Ops:
  0.7 53.0 %copy-start = (bf16[128,1024]{1,0:T(8,128)(2,1)S(1)}, bf16[128,1024]{1,0:T(8,128)(2,1)}, u32[]{:S(2)}) copy-start(bf16[128,1024]{1,0:T(8,128)(2,1)} %param.13) | copy-start | bytes 786436
  0.7 53.0 %copy-start.1 = (bf16[128,1024]{1,0:T(8,128)(2,1)S(1)}, bf16[128,1024]{1,0:T(8,128)(2,1)}, u32[]{:S(2)}) copy-start(bf16[128,1024]{1,0:T(8,128)(2,1)} %param.12) | copy-start | bytes 786436
